TPU v7x, 32 devices: a whole 2x2x4 slice. The times are simulated.
32 devices in a mesh: stream: 2 (over y), docs: 16 (over z, x, core).
Axes of the slice: x: 2, y: 2, z: 4, core: 2. Of those that a mesh axis runs over, the one named last changes fastest.
Arguments:
- block_features: bfloat16 [2, 8192, 768], P('stream', 'docs'), may hold values from -6 to 6
- cotangent: bfloat16 [2, 8192, 768], P('stream', 'docs'), may hold values from -6 to 6
- text_counts: int32 [16, 2], P('docs'), may hold values from 64 to 448, as said below
- visual_counts: int32 [16, 2], P('docs'), may hold values from 1 to 89, as said below
- w_cross_q: bfloat16 [2, 768, 768], P('stream'), may hold values from -0.21875 to 0.21875
- w_cross_kv: bfloat16 [2, 768, 1536], P('stream'), may hold values from -0.21875 to 0.21875
- w_cross_out: bfloat16 [2, 768, 768], P('stream'), may hold values from -1.25 to 1.25
- w_self_qkv: bfloat16 [2, 768, 2304], P('stream'), may hold values from -0.21875 to 0.21875
- w_self_out: bfloat16 [2, 768, 768], P('stream'), may hold values from -1.75 to 1.75
- w_ffn_in: bfloat16 [2, 768, 3072], P('stream'), may hold values from -0.21875 to 0.21875
- w_ffn_out: bfloat16 [2, 3072, 768], P('stream'), may hold values from -0.109375 to 0.109375
- w_gate: bfloat16 [2, 1536, 768], P('stream'), may hold values from -0.15625 to 0.15625
- ln_gain: bfloat16 [2, 3, 768], P('stream'), may hold values from 0.5 to 1.5
- ln_bias: bfloat16 [2, 3, 768], P('stream'), may hold values from -3 to 3
- gate_bias: bfloat16 [2, 768], P('stream'), may hold values from -3 to 3
Outputs:
- combined: float32 [2, 8192, 768], P('stream', 'docs')
- input_grad: float32 [2, 8192, 768], P('stream', 'docs')
- grad_cross_q: float32 [2, 768, 768], P('stream', 'docs')
- grad_cross_kv: float32 [2, 768, 1536], P('stream', 'docs')
- grad_cross_out: float32 [2, 768, 768], P('stream', 'docs')
- grad_self_qkv: float32 [2, 768, 2304], P('stream', 'docs')
- grad_self_out: float32 [2, 768, 768], P('stream', 'docs')
- grad_ffn_in: float32 [2, 768, 3072], P('stream', 'docs')
- grad_ffn_out: float32 [2, 3072, 768], P('stream', 'docs')
- grad_gate: float32 [2, 1536, 768], P('stream', 'docs')
- grad_ln_gain: float32 [2, 3, 768], P('stream', None, 'docs')
- grad_ln_bias: float32 [2, 3, 768], P('stream', None, 'docs')
- grad_gate_bias: float32 [2, 768], P('stream', 'docs')
Inputs may be any that keep to these rules, and one draw needn't show every extreme that they name: `text_counts`: the 2 text counts of one group of 512 rows sum to 512. `visual_counts`: each document has at least one visual block and no more visual blocks than text blocks.
All inputs are finite; a program needn't handle non-finite values.
Results may differ from a plain program's by a relative error of at most 0.025.
Values may be sent and summed in bfloat16 or wider, within the bound.
No kernel may reach another device: no remote copies, remote signals or barrier semaphores. Data moves between devices by JAX's collectives and lax.ppermute only.
A program may use at most 192 MiB of HBM per device.

v0:
```python
import jax
import jax.numpy as jnp
from jax import lax
from jax.sharding import PartitionSpec as P

HD = 64


norm_epsilon = 1e-06
masked_value = -1e30


def from_partner(shard, axis, distance):
    return lax.ppermute(shard, axis, [(i, i ^ 1 << distance) for i in range(lax.axis_size(axis))])


def layer_norm(resid, gain, shift):
    center = resid - jnp.mean(resid, axis=-1, keepdims=True)
    spread = jnp.mean(center * center, axis=-1, keepdims=True)
    return center * lax.rsqrt(spread + norm_epsilon) * gain + shift


def gelu_exact(values):
    return jax.nn.gelu(values, approximate=False)


def times_transposed(left, right):
    return lax.dot_general(
        left, right, (((1,), (1,)), ((), ())), preferred_element_type=jnp.float32
    )


def outer_sum(left, right):
    return lax.dot_general(
        left, right, (((0,), (0,)), ((), ())), preferred_element_type=jnp.float32
    )


def owner_pieces(term, doc_count):
    return term.reshape((doc_count, term.shape[0] // doc_count) + term.shape[1:])


def add_pieces(received):
    return tuple((jnp.sum(piece, axis=0) for piece in received))


def layout(text_row, visual_row, tokens):
    doc_ends = jnp.cumsum(text_row)
    doc_starts = doc_ends - text_row
    positions = jnp.arange(tokens, dtype=jnp.int32)
    doc_ids = jnp.sum((positions[:, None] >= doc_ends[None, :]).astype(jnp.int32), axis=1)
    member = doc_ids[:, None] == jnp.arange(text_row.shape[0], dtype=jnp.int32)[None, :]
    row_start = jnp.sum(jnp.where(member, doc_starts[None, :], 0), axis=1)
    row_visual = jnp.sum(jnp.where(member, visual_row[None, :], 0), axis=1)
    visible = positions - row_start < row_visual
    return (doc_ids, visible)


def split_heads(rows):
    return rows.reshape(rows.shape[0], rows.shape[1] // HD, HD)


def block_scores(query_block, key_heads, doc_ids, key_valid):
    allowed = (doc_ids[:, None] == doc_ids[None, :]) & key_valid[None, :]
    raw = jnp.einsum(
        "qhd,khd->hqk", query_block, key_heads, preferred_element_type=jnp.float32
    ) * HD ** (-0.5)
    return jnp.where(allowed[None], raw, masked_value)


def attend(queries, key_rows, value_rows, doc_ids, key_valid):
    tokens = queries.shape[0]
    query_heads = split_heads(queries)
    key_heads = split_heads(key_rows)
    value_heads = split_heads(value_rows)
    scores = block_scores(query_heads, key_heads, doc_ids, key_valid)
    row_max = jnp.max(scores, axis=-1, keepdims=True)
    shifted = jnp.exp(scores - row_max)
    row_total = jnp.sum(shifted, axis=-1, keepdims=True)
    attn_probs = (shifted / row_total).astype(jnp.bfloat16)
    results = jnp.einsum(
        "hqk,khd->qhd", attn_probs, value_heads, preferred_element_type=jnp.float32
    )
    log_sums = [row_max + jnp.log(row_total)]
    return (results.reshape(tokens, -1), log_sums)


def attend_back(queries, key_rows, value_rows, out_grad, log_sums, doc_ids, key_valid):
    tokens = queries.shape[0]
    block_rows = min(512, tokens)
    query_heads = split_heads(queries)
    key_heads = split_heads(key_rows)
    value_heads = split_heads(value_rows)
    out_heads = split_heads(out_grad)
    score_scale = HD ** (-0.5)
    query_grads = []
    key_grad = jnp.zeros(key_heads.shape, jnp.float32)
    value_grad = jnp.zeros(value_heads.shape, jnp.float32)
    for block_index, row_start in enumerate(range(0, tokens, block_rows)):
        scores = block_scores(query_heads, key_heads, doc_ids, key_valid)
        attn_probs = jnp.exp(scores - log_sums[block_index])
        prob_grad = jnp.einsum(
            "qhd,khd->hqk", out_heads, value_heads, preferred_element_type=jnp.float32
        )
        inner = jnp.sum(attn_probs * prob_grad, axis=-1, keepdims=True)
        score_grad = (attn_probs * (prob_grad - inner)).astype(jnp.bfloat16)
        query_grads.append(
            jnp.einsum("hqk,khd->qhd", score_grad, key_heads, preferred_element_type=jnp.float32)
            * score_scale
        )
        key_grad = (
            jnp.einsum("hqk,qhd->khd", score_grad, query_heads, preferred_element_type=jnp.float32)
            * score_scale
        )
        value_grad = jnp.einsum(
            "hqk,qhd->khd",
            attn_probs.astype(jnp.bfloat16),
            out_heads,
            preferred_element_type=jnp.float32,
        )
    query_grad = query_grads[0].reshape(tokens, -1)
    return (query_grad, key_grad.reshape(tokens, -1), value_grad.reshape(tokens, -1))


def body(
    block_features,
    cotangent,
    text_counts,
    visual_counts,
    w_cross_q,
    w_cross_kv,
    w_cross_out,
    w_self_qkv,
    w_self_out,
    w_ffn_in,
    w_ffn_out,
    w_gate,
    ln_gain,
    ln_bias,
    gate_bias,
):
    features = block_features[0]
    cot_rows = cotangent[0].astype(jnp.float32)
    tokens = features.shape[0]
    model_width = features.shape[1]
    doc_count = lax.axis_size("docs")
    half_index = lax.axis_index("stream")
    doc_ids, visible = layout(text_counts[0], visual_counts[0], tokens)
    visible_float = visible.astype(jnp.float32)
    own_valid = jnp.where(half_index == 0, jnp.ones_like(visible_float), visible_float)
    other_valid = jnp.where(half_index == 0, visible_float, jnp.ones_like(visible_float))
    own_keys = own_valid > 0.5
    other_keys = other_valid > 0.5
    cross_q = w_cross_q[0]
    cross_kv = w_cross_kv[0]
    cross_out = w_cross_out[0]
    self_qkv_w = w_self_qkv[0]
    self_out_w = w_self_out[0]
    ffn_in = w_ffn_in[0]
    ffn_out = w_ffn_out[0]
    gate_w = w_gate[0]
    gains = ln_gain[0].astype(jnp.float32)
    shifts = ln_bias[0].astype(jnp.float32)
    gate_shift = gate_bias[0].astype(jnp.float32)
    own_kv = jnp.dot(features, cross_kv, preferred_element_type=jnp.float32).astype(jnp.bfloat16)
    partner_kv = from_partner(own_kv, "stream", 0)
    queries = jnp.dot(features, cross_q, preferred_element_type=jnp.float32).astype(jnp.bfloat16)
    cross_res, cross_sums = attend(
        queries, partner_kv[:, :model_width], partner_kv[:, model_width:], doc_ids, other_keys
    )
    cross_low = cross_res.astype(jnp.bfloat16)
    first_in = features.astype(jnp.float32) + jnp.dot(
        cross_low, cross_out, preferred_element_type=jnp.float32
    )
    first_out, first_pull = jax.vjp(layer_norm, first_in, gains[0], shifts[0])
    first_low = first_out.astype(jnp.bfloat16)
    self_qkv = jnp.dot(first_low, self_qkv_w, preferred_element_type=jnp.float32).astype(
        jnp.bfloat16
    )
    self_queries = self_qkv[:, :model_width]
    self_keys = self_qkv[:, model_width : 2 * model_width]
    self_values = self_qkv[:, 2 * model_width :]
    self_res, self_sums = attend(self_queries, self_keys, self_values, doc_ids, own_keys)
    self_low = self_res.astype(jnp.bfloat16)
    second_in = first_out + jnp.dot(self_low, self_out_w, preferred_element_type=jnp.float32)
    second, second_pull = jax.vjp(layer_norm, second_in, gains[1], shifts[1])
    second_low = second.astype(jnp.bfloat16)
    pre_act = jnp.dot(second_low, ffn_in, preferred_element_type=jnp.float32)
    activated, gelu_pull = jax.vjp(gelu_exact, pre_act)
    hidden = activated.astype(jnp.bfloat16)
    third_in = second + jnp.dot(hidden, ffn_out, preferred_element_type=jnp.float32)
    third_raw, third_pull = jax.vjp(layer_norm, third_in, gains[2], shifts[2])
    third_out = third_raw * own_valid[:, None]
    third_low = third_out.astype(jnp.bfloat16)
    partner_third = from_partner(third_low, "stream", 0)
    gate_in = jnp.concatenate([third_low, partner_third], axis=1)
    gate_value = jax.nn.sigmoid(
        jnp.dot(gate_in, gate_w, preferred_element_type=jnp.float32) + gate_shift
    )
    partner_float = partner_third.astype(jnp.float32)
    combined = own_valid[:, None] * (gate_value * third_out + (1.0 - gate_value) * partner_float)
    out_grad = cot_rows * own_valid[:, None]
    gate_grad = out_grad * (third_out - partner_float)
    logit_grad = gate_grad * gate_value * (1.0 - gate_value)
    grad_gate_shift = jnp.sum(logit_grad, axis=0)
    logit_low = logit_grad.astype(jnp.bfloat16)
    grad_gate_w = outer_sum(gate_in, logit_low)
    gate_in_grad = times_transposed(logit_low, gate_w)
    partner_grad = gate_in_grad[:, model_width:] + out_grad * (1.0 - gate_value)
    returned_third = from_partner(partner_grad.astype(jnp.bfloat16), "stream", 0)
    third_grad = (
        out_grad * gate_value + gate_in_grad[:, :model_width] + returned_third.astype(jnp.float32)
    ) * own_valid[:, None]
    third_in_grad, gain_grad_c, shift_grad_c = third_pull(third_grad)
    third_in_low = third_in_grad.astype(jnp.bfloat16)
    grad_ffn_out_w = outer_sum(hidden, third_in_low)
    hidden_grad = times_transposed(third_in_low, ffn_out)
    (pre_grad,) = gelu_pull(hidden_grad)
    pre_low = pre_grad.astype(jnp.bfloat16)
    grad_ffn_in_w = outer_sum(second_low, pre_low)
    second_grad = third_in_grad + times_transposed(pre_low, ffn_in)
    second_in_grad, gain_grad_b, shift_grad_b = second_pull(second_grad)
    second_in_low = second_in_grad.astype(jnp.bfloat16)
    grad_self_out_w = outer_sum(self_low, second_in_low)
    self_res_grad = times_transposed(second_in_low, self_out_w).astype(jnp.bfloat16)
    self_q_grad, self_k_grad, self_v_grad = attend_back(
        self_queries, self_keys, self_values, self_res_grad, self_sums, doc_ids, own_keys
    )
    qkv_low = jnp.concatenate([self_q_grad, self_k_grad, self_v_grad], axis=1).astype(jnp.bfloat16)
    grad_self_qkv_w = outer_sum(first_low, qkv_low)
    first_grad = second_in_grad + times_transposed(qkv_low, self_qkv_w)
    first_in_grad, gain_grad_a, shift_grad_a = first_pull(first_grad)
    first_in_low = first_in_grad.astype(jnp.bfloat16)
    grad_cross_out_w = outer_sum(cross_low, first_in_low)
    cross_res_grad = times_transposed(first_in_low, cross_out).astype(jnp.bfloat16)
    partner_again = from_partner(own_kv, "stream", 0)
    cross_q_grad, partner_k_grad, partner_v_grad = attend_back(
        queries,
        partner_again[:, :model_width],
        partner_again[:, model_width:],
        cross_res_grad,
        cross_sums,
        doc_ids,
        other_keys,
    )
    partner_kv_grad = jnp.concatenate([partner_k_grad, partner_v_grad], axis=1).astype(jnp.bfloat16)
    returned_kv = from_partner(partner_kv_grad, "stream", 0)
    cross_q_low = cross_q_grad.astype(jnp.bfloat16)
    grad_cross_q_w = outer_sum(features, cross_q_low)
    grad_cross_kv_w = outer_sum(features, returned_kv)
    feature_grad = (
        first_in_grad
        + times_transposed(cross_q_low, cross_q)
        + times_transposed(returned_kv, cross_kv)
    )
    gain_grads = jnp.stack([gain_grad_a, gain_grad_b, gain_grad_c])
    shift_grads = jnp.stack([shift_grad_a, shift_grad_b, shift_grad_c])
    small_cols = jnp.concatenate([gain_grads, shift_grads, grad_gate_shift[None]], axis=0).T
    all_parts = (
        lax.all_to_all(
            owner_pieces(grad_cross_q_w, doc_count).astype(jnp.bfloat16),
            "docs",
            split_axis=0,
            concat_axis=0,
            tiled=True,
        ).astype(jnp.float32),
        lax.all_to_all(
            owner_pieces(grad_cross_kv_w, doc_count).astype(jnp.bfloat16),
            "docs",
            split_axis=0,
            concat_axis=0,
            tiled=True,
        ).astype(jnp.float32),
        lax.all_to_all(
            owner_pieces(grad_cross_out_w, doc_count).astype(jnp.bfloat16),
            "docs",
            split_axis=0,
            concat_axis=0,
            tiled=True,
        ).astype(jnp.float32),
        lax.all_to_all(
            owner_pieces(grad_self_qkv_w, doc_count).astype(jnp.bfloat16),
            "docs",
            split_axis=0,
            concat_axis=0,
            tiled=True,
        ).astype(jnp.float32),
        lax.all_to_all(
            owner_pieces(grad_self_out_w, doc_count).astype(jnp.bfloat16),
            "docs",
            split_axis=0,
            concat_axis=0,
            tiled=True,
        ).astype(jnp.float32),
        lax.all_to_all(
            owner_pieces(grad_ffn_in_w, doc_count).astype(jnp.bfloat16),
            "docs",
            split_axis=0,
            concat_axis=0,
            tiled=True,
        ).astype(jnp.float32),
        lax.all_to_all(
            owner_pieces(grad_ffn_out_w, doc_count).astype(jnp.bfloat16),
            "docs",
            split_axis=0,
            concat_axis=0,
            tiled=True,
        ).astype(jnp.float32),
        lax.all_to_all(
            owner_pieces(grad_gate_w, doc_count).astype(jnp.bfloat16),
            "docs",
            split_axis=0,
            concat_axis=0,
            tiled=True,
        ).astype(jnp.float32),
        lax.all_to_all(
            owner_pieces(small_cols, doc_count).astype(jnp.bfloat16),
            "docs",
            split_axis=0,
            concat_axis=0,
            tiled=True,
        ).astype(jnp.float32),
    )
    (
        summed_cross_q,
        summed_cross_kv,
        summed_cross_out,
        summed_self_qkv,
        summed_self_out,
        summed_ffn_in,
        summed_ffn_out,
        summed_gate_w,
        summed_small,
    ) = add_pieces(all_parts)
    summed_rows = summed_small.T
    summed_gains = summed_rows[0:3]
    summed_shifts = summed_rows[3:6]
    summed_gate_shift = summed_rows[6]
    return (
        combined[None],
        feature_grad[None],
        summed_cross_q[None],
        summed_cross_kv[None],
        summed_cross_out[None],
        summed_self_qkv[None],
        summed_self_out[None],
        summed_ffn_in[None],
        summed_ffn_out[None],
        summed_gate_w[None],
        summed_gains[None],
        summed_shifts[None],
        summed_gate_shift[None],
    )


def solution(mesh):
    in_specs = (
        P("stream", "docs", None),
        P("stream", "docs", None),
        P("docs", None),
        P("docs", None),
        P("stream", None, None),
        P("stream", None, None),
        P("stream", None, None),
        P("stream", None, None),
        P("stream", None, None),
        P("stream", None, None),
        P("stream", None, None),
        P("stream", None, None),
        P("stream", None, None),
        P("stream", None, None),
        P("stream", None),
    )
    out_specs = (
        P("stream", "docs", None),
        P("stream", "docs", None),
        P("stream", "docs", None),
        P("stream", "docs", None),
        P("stream", "docs", None),
        P("stream", "docs", None),
        P("stream", "docs", None),
        P("stream", "docs", None),
        P("stream", "docs", None),
        P("stream", "docs", None),
        P("stream", None, "docs"),
        P("stream", None, "docs"),
        P("stream", "docs"),
    )
    return jax.shard_map(body, mesh=mesh, in_specs=in_specs, out_specs=out_specs, check_vma=False)
```

profile of v0, /device:TPU:15, one launch (start us, length us, event | category | flops | bytes accessed | tf_op | source)
XLA Modules:
  0.0 752.0 jit_solution(14705170224691783850)
XLA Ops:
  0.7 4.6 convolution_convert_fusion.6
  9.8 2.3 copy.102
  16.3 24.6 %collective-permute-done = bf16[512,1536]{1,0:T(8,128)(2,1)} collective-permute-done((bf16[512,1536]{1,0:T(8,128)(2,1)}, bf16[512,1536]{1,0:T(8,128)(2,1)}, u32[]{:S(2)}, u32[]{:S(2)}) %collective-permute-start) | collective-permute-done | bytes 1572896 | tf_op jit(solution)/shard_map/ppermute | solution.py:14
  40.9 2.6 fusion.118
  43.5 2.3 copy.103
  45.8 2.3 copy.101
  48.1 3.5 fusion.26
  51.6 3.7 fusion
  56.3 5.0 fusion.69
  63.5 2.1 convolution_convert_fusion.3
  67.1 2.3 copy.107
  69.4 2.3 copy.106
  71.7 2.3 copy.105
  74.0 3.5 fusion.27
  77.5 3.7 fusion.1
  82.0 5.3 fusion.68
  88.9 19.9 %multiply_convert_fusion.2 = (bf16[512,3072]{1,0:T(8,128)(2,1)S(1)}, f32[512,3072]{1,0:T(8,128)}, f32[512,3072]{1,0:T(8,128)}) fusion(bf16[1,768,3072]{2,1,0:T(8,128)(2,1)} %param.24, f32[512,768]{1,0:T(8,128)S(1)} %get-tuple-element.60, f32[768]{0:T(1024)S(1)} %copy-done.45, f32[768]{0:T(1024)S(1)} %copy-done.37, f32[512]{0:T(512)S(1)} %fusion.90, ...), kind=kOutput, calls=%fused_computation.26 | convolution fusion | flops 2520121344 | bytes 22030336 | tf_op jit(solution)/shard_map/dot_general | solution.py:188
  110.4 2.7 fusion.122
  114.2 17.2 %collective-permute-done.1 = bf16[512,768]{1,0:T(8,128)(2,1)S(1)} collective-permute-done((bf16[512,768]{1,0:T(8,128)(2,1)S(1)}, bf16[512,768]{1,0:T(8,128)(2,1)S(1)}, u32[]{:S(2)}, u32[]{:S(2)}) %collective-permute-start.1) | collective-permute-done | bytes 786464 | tf_op jit(solution)/shard_map/ppermute | solution.py:14
  133.0 2.4 fusion.110
  138.6 15.1 %collective-permute-done.2 = bf16[512,768]{1,0:T(8,128)(2,1)S(1)} collective-permute-done((bf16[512,768]{1,0:T(8,128)(2,1)S(1)}, bf16[512,768]{1,0:T(8,128)(2,1)S(1)}, u32[]{:S(2)}, u32[]{:S(2)}) %collective-permute-start.2) | collective-permute-done | bytes 786464 | tf_op jit(solution)/shard_map/ppermute | solution.py:14
  156.0 8.9 %add_convert_fusion = bf16[512,3072]{1,0:T(8,128)(2,1)} fusion(f32[512,3072]{1,0:T(8,128)} %get-tuple-element.40, f32[512,3072]{1,0:T(8,128)} %get-tuple-element.61, bf16[1,3072,768]{2,1,0:T(8,128)(2,1)S(1)} %bitcast.250, f32[512,768]{1,0:T(8,128)S(1)} %get-tuple-element.37, f32[512]{0:T(512)S(1)} %negate_multiply_fusion.3), kind=kOutput, calls=%fused_computation.25 | convolution fusion | flops 2438725632 | bytes 22022144 | tf_op jit(solution)/shard_map/dot_general | solution.py:28
  164.9 5.6 multiply_reduce_fusion.3
  174.2 2.3 copy.109
  176.5 8.1 %fusion.62 = bf16[12,64,512]{2,1,0:T(8,128)(2,1)S(1)} fusion(bf16[512,12,64]{0,2,1:T(8,128)(2,1)} %bitcast.222, f32[12,512]{1,0:T(8,128)} %log_add_fusion.1, f32[12,512,512]{1,2,0:T(8,128)} %copy-done.2, pred[512,512]{0,1:T(8,128)(4,1)} %get-tuple-element.51), kind=kOutput, calls=%fused_computation.128 | convolution fusion | flops 415629312 | bytes 14442496 | tf_op jit(solution)/shard_map/hqk,qhd->khd/dot_general | solution.py:115
  184.7 9.8 %multiply_reduce_fusion.1 = (f32[12,512]{1,0:T(8,128)S(1)}, f32[12,512,512]{1,2,0:T(8,128)}) fusion(f32[12,512]{1,0:T(8,128)S(1)} %copy-done.31, f32[12,512,512]{1,2,0:T(8,128)} %copy-done.2, pred[512,512]{0,1:T(8,128)(4,1)S(1)} %copy-done.10, bf16[512,12,64]{0,2,1:T(8,128)(2,1)S(1)} %bitcast.223, bf16[512,12,64]{0,2,1:T(8,128)(2,1)S(1)} %bitcast.219), kind=kOutput, calls=%fused_computation.4 | convolution fusion | flops 418375680 | bytes 27049984 | tf_op jit(solution)/shard_map/qhd,khd->hqk/dot_general | solution.py:102
  194.5 7.3 multiply_convert_fusion.1
  207.5 4.4 multiply_reduce_fusion.4
  216.8 9.3 %all-to-all-start.8 = ((bf16[16,2,168]{2,1,0:T(2,128)(2,1)}), bf16[16,2,168]{2,1,0:T(2,128)(2,1)S(1)}, u32[]{:S(2)}, u32[]{:S(2)}) async-start(bf16[16,2,168]{2,1,0:T(2,128)(2,1)} %reshape.394), calls=%async_computation.8 | async-start | bytes 32768 | tf_op jit(solution)/shard_map/all_to_all | solution.py:316
  226.1 3.5 convolution_convert_fusion.7
  230.2 6.6 all-to-all-start.4
  238.9 2.6 fusion.112
  244.4 2.3 copy.113
  246.7 3.5 convolution_convert_fusion.8
  250.3 14.4 %all-to-all-done.4 = bf16[16,48,768]{2,1,0:T(8,128)(2,1)} async-done(((bf16[16,48,768]{2,1,0:T(8,128)(2,1)}), bf16[16,48,768]{2,1,0:T(8,128)(2,1)}, u32[]{:S(2)}, u32[]{:S(2)}) %all-to-all-start.4) | async-done | bytes 1179680 | tf_op jit(solution)/shard_map/all_to_all | solution.py:288
  264.7 5.2 all-to-all-start.2
  270.0 13.5 %multiply_reduce_fusion = (f32[12,512]{1,0:T(8,128)S(1)}, f32[12,512,512]{1,2,0:T(8,128)}) fusion(f32[12,512]{1,0:T(8,128)} %log_add_fusion, f32[12,512,512]{1,2,0:T(8,128)} %copy-done.1, pred[512,512]{0,1:T(8,128)(4,1)} %get-tuple-element.52, bf16[512,12,64]{0,2,1:T(8,128)(2,1)} %bitcast.220, bf16[512,12,64]{0,2,1:T(8,128)(2,1)} %bitcast.217), kind=kOutput, calls=%fused_computation.1 | convolution fusion | flops 418375680 | bytes 27049984 | tf_op jit(solution)/shard_map/qhd,khd->hqk/dot_general | solution.py:102
  283.5 7.1 multiply_convert_fusion
  297.6 4.9 all-to-all-start
  302.5 4.5 convolution_convert_fusion.4
  307.0 23.4 %all-to-all-done = bf16[16,48,768]{2,1,0:T(8,128)(2,1)} async-done(((bf16[16,48,768]{2,1,0:T(8,128)(2,1)}), bf16[16,48,768]{2,1,0:T(8,128)(2,1)}, u32[]{:S(2)}, u32[]{:S(2)}) %all-to-all-start) | async-done | bytes 1179680 | tf_op jit(solution)/shard_map/all_to_all | solution.py:260
  330.4 5.5 all-to-all-start.7
  335.9 5.1 multiply_convert_fusion.3
  341.0 6.3 fusion.65
  347.7 35.4 %collective-permute-done.3 = bf16[512,1536]{0,1:T(8,128)(2,1)S(1)} collective-permute-done((bf16[512,1536]{0,1:T(8,128)(2,1)S(1)}, bf16[512,1536]{0,1:T(8,128)(2,1)S(1)}, u32[]{:S(2)}, u32[]{:S(2)}) %collective-permute-start.3) | collective-permute-done | bytes 1572896 | tf_op jit(solution)/shard_map/ppermute | solution.py:14
  384.3 2.9 convolution_convert_fusion.5
  388.8 5.3 all-to-all-start.1
  394.1 6.2 convolution_convert_fusion.2
  400.3 47.0 %all-to-all-done.1 = bf16[16,48,1536]{2,1,0:T(8,128)(2,1)} async-done(((bf16[16,48,1536]{2,1,0:T(8,128)(2,1)}), bf16[16,48,1536]{2,1,0:T(8,128)(2,1)}, u32[]{:S(2)}, u32[]{:S(2)}) %all-to-all-start.1) | async-done | bytes 2359328 | tf_op jit(solution)/shard_map/all_to_all | solution.py:267
  447.2 4.9 all-to-all-start.3
  452.1 7.5 convolution_convert_fusion.1
  459.6 70.9 %all-to-all-done.3 = bf16[16,48,2304]{2,1,0:T(8,128)(2,1)} async-done(((bf16[16,48,2304]{2,1,0:T(8,128)(2,1)}), bf16[16,48,2304]{2,1,0:T(8,128)(2,1)}, u32[]{:S(2)}, u32[]{:S(2)}) %all-to-all-start.3) | async-done | bytes 3538976 | tf_op jit(solution)/shard_map/all_to_all | solution.py:281
  530.6 5.2 all-to-all-start.5
  535.8 7.3 convolution_convert_fusion
  543.1 96.3 %all-to-all-done.5 = bf16[16,48,3072]{2,1,0:T(8,128)(2,1)} async-done(((bf16[16,48,3072]{2,1,0:T(8,128)(2,1)}), bf16[16,48,3072]{2,1,0:T(8,128)(2,1)}, u32[]{:S(2)}, u32[]{:S(2)}) %all-to-all-start.5) | async-done | bytes 4718624 | tf_op jit(solution)/shard_map/all_to_all | solution.py:295
  639.4 4.9 all-to-all-start.6
  644.2 3.5 fusion.76
  650.9 5.8 add_bitcast_fusion
  662.9 2.7 convert_reduce_fusion.3
  665.6 2.7 convert_reduce_fusion.4
  668.4 3.3 convert_reduce_fusion.2
  671.7 4.1 convert_reduce_fusion.1
  675.8 72.2 %all-to-all-done.6 = bf16[16,192,768]{2,1,0:T(8,128)(2,1)} async-done(((bf16[16,192,768]{2,1,0:T(8,128)(2,1)}), bf16[16,192,768]{2,1,0:T(8,128)(2,1)}, u32[]{:S(2)}, u32[]{:S(2)}) %all-to-all-start.6) | async-done | bytes 4718624 | tf_op jit(solution)/shard_map/all_to_all | solution.py:302
  747.9 3.9 convert_reduce_fusion
  (238 shorter events, 64.1 us)
Async XLA Ops:
  0.6 62.8 %copy-start = (bf16[1,768,2304]{2,1,0:T(8,128)(2,1)S(1)}, bf16[1,768,2304]{2,1,0:T(8,128)(2,1)}, u32[]{:S(2)}) copy-start(bf16[1,768,2304]{2,1,0:T(8,128)(2,1)} %param.22) | copy-start | bytes 10616836
  0.7 4.8 copy-start.61
  0.7 4.8 copy-start.60
  5.3 8.3 %copy-start.53 = (s32[1,2]{1,0:T(1,128)S(1)}, s32[1,2]{1,0:T(1,128)}, u32[]{:S(2)}) copy-start(s32[1,2]{1,0:T(1,128)} %param.18) | copy-start | bytes 28
  5.3 35.6 %collective-permute-start = (bf16[512,1536]{1,0:T(8,128)(2,1)}, bf16[512,1536]{1,0:T(8,128)(2,1)}, u32[]{:S(2)}, u32[]{:S(2)}) collective-permute-start(bf16[512,1536]{1,0:T(8,128)(2,1)} %convolution_convert_fusion.6), channel_id=1, source_target_pairs={{0,16},{16,0},{1,17},{17,1},{2,18},{18,2},{3,19},{19,3},{4,20},{20... | collective-permute-start | bytes 4718600 | tf_op jit(solution)/shard_map/ppermute | solution.py:14
  51.6 4.6 copy-start.1
  51.6 4.7 copy-start.28
  55.3 6.0 copy-start.32
  56.3 5.1 copy-start.58
  56.3 5.1 copy-start.62
  62.4 145.1 %copy-start.34 = (f32[512]{0:T(512)}, f32[512]{0:T(512)S(1)}, u32[]{:S(2)}) copy-start(f32[512]{0:T(512)S(1)} %broadcast_multiply_fusion.2) | copy-start | bytes 6148
  77.5 4.5 copy-start.2
  82.0 5.4 copy-start.12
  82.0 5.4 copy-start.40
  82.0 5.4 copy-start.47
  82.0 5.4 copy-start.56
  87.4 22.9 %slice-start.6 = ((s8[4718592]{0:T(1024)(128)(4,1)}), s8[4194304]{0:T(1024)(128)(4,1)S(1)}, s32[]{:S(2)}) async-start(s8[4718592]{0:T(1024)(128)(4,1)} %bitcast.249), calls=%async_computation.15 | async-start | bytes 8388608
  88.5 82.1 %copy-start.14 = (f32[512,768]{1,0:T(8,128)}, f32[512,768]{1,0:T(8,128)S(1)}, u32[]{:S(2)}) copy-start(f32[512,768]{1,0:T(8,128)S(1)} %get-tuple-element.60) | copy-start | bytes 4718596
  88.5 82.1 %copy-start.35 = (f32[512]{0:T(512)}, f32[512]{0:T(512)S(1)}, u32[]{:S(2)}) copy-start(f32[512]{0:T(512)S(1)} %broadcast_multiply_fusion.1) | copy-start | bytes 6148
  88.8 81.8 %copy-start.42 = (f32[512]{0:T(512)}, f32[512]{0:T(512)S(1)}, u32[]{:S(2)}) copy-start(f32[512]{0:T(512)S(1)} %fusion.90) | copy-start | bytes 6148
  88.9 21.5 %slice-start.7 = ((s8[4718592]{0:T(1024)(128)(4,1)}), s8[524288]{0:T(1024)(128)(4,1)S(1)}, s32[]{:S(2)}) async-start(s8[4718592]{0:T(1024)(128)(4,1)} %bitcast.249), calls=%async_computation.16 | async-start | bytes 1048576
  113.1 18.3 %copy-start.54 = (bf16[1,1536,768]{2,1,0:T(8,128)(2,1)S(1)}, bf16[1,1536,768]{2,1,0:T(8,128)(2,1)}, u32[]{:S(2)}) copy-start(bf16[1,1536,768]{2,1,0:T(8,128)(2,1)} %param.26) | copy-start | bytes 7077892
  113.8 17.6 %copy-start.26 = (bf16[512,768]{1,0:T(8,128)(2,1)}, bf16[512,768]{1,0:T(8,128)(2,1)S(1)}, u32[]{:S(2)}) copy-start(bf16[512,768]{1,0:T(8,128)(2,1)S(1)} %fusion.109) | copy-start | bytes 2359300
  113.9 17.6 %collective-permute-start.1 = (bf16[512,768]{1,0:T(8,128)(2,1)S(1)}, bf16[512,768]{1,0:T(8,128)(2,1)S(1)}, u32[]{:S(2)}, u32[]{:S(2)}) collective-permute-start(bf16[512,768]{1,0:T(8,128)(2,1)S(1)} %fusion.109), channel_id=1, source_target_pairs={{0,16},{16,0},{1,17},{17,1},{2,18},{18,2},{3,19},{19,3},{4,20},{20... | collective-permute-start | bytes 2359304 | tf_op jit(solution)/shard_map/ppermute | solution.py:14
  114.2 18.8 %copy-start.7 = (bf16[1,512,768]{2,1,0:T(8,128)(2,1)S(1)}, bf16[1,512,768]{2,1,0:T(8,128)(2,1)}, u32[]{:S(2)}) copy-start(bf16[1,512,768]{2,1,0:T(8,128)(2,1)} %param.16) | copy-start | bytes 2359300
  137.1 16.6 %collective-permute-start.2 = (bf16[512,768]{1,0:T(8,128)(2,1)S(1)}, bf16[512,768]{1,0:T(8,128)(2,1)S(1)}, u32[]{:S(2)}, u32[]{:S(2)}) collective-permute-start(bf16[512,768]{1,0:T(8,128)(2,1)S(1)} %fusion.46), channel_id=1, source_target_pairs={{0,16},{16,0},{1,17},{17,1},{2,18},{18,2},{3,19},{19,3},{4,20},{20... | collective-permute-start | bytes 2359304 | tf_op jit(solution)/shard_map/ppermute | solution.py:14
  153.8 11.1 %slice-start.8 = ((s8[4718592]{0:T(1024)(128)(4,1)}), s8[4194304]{0:T(1024)(128)(4,1)S(1)}, s32[]{:S(2)}) async-start(s8[4718592]{0:T(1024)(128)(4,1)} %bitcast.251), calls=%async_computation.17 | async-start | bytes 8388608
  155.9 9.0 %copy-start.20 = (f32[512,768]{1,0:T(8,128)}, f32[512,768]{1,0:T(8,128)S(1)}, u32[]{:S(2)}) copy-start(f32[512,768]{1,0:T(8,128)S(1)} %get-tuple-element.37) | copy-start | bytes 4718596
  155.9 8.9 %copy-start.49 = (f32[512]{0:T(512)}, f32[512]{0:T(512)S(1)}, u32[]{:S(2)}) copy-start(f32[512]{0:T(512)S(1)} %negate_multiply_fusion.3) | copy-start | bytes 6148
  156.0 9.0 %slice-start.9 = ((s8[4718592]{0:T(1024)(128)(4,1)}), s8[524288]{0:T(1024)(128)(4,1)S(1)}, s32[]{:S(2)}) async-start(s8[4718592]{0:T(1024)(128)(4,1)} %bitcast.251), calls=%async_computation.18 | async-start | bytes 1048576
  171.3 36.2 %copy-start.51 = (f32[512]{0:T(512)}, f32[512]{0:T(512)S(1)}, u32[]{:S(2)}) copy-start(f32[512]{0:T(512)S(1)} %negate_multiply_fusion.2) | copy-start | bytes 6148
  176.5 8.1 %copy-start.10 = (pred[512,512]{0,1:T(8,128)(4,1)S(1)}, pred[512,512]{0,1:T(8,128)(4,1)}, u32[]{:S(2)}) copy-start(pred[512,512]{0,1:T(8,128)(4,1)} %get-tuple-element.51) | copy-start | bytes 786436
  176.5 8.1 %copy-start.15 = (bf16[512,768]{0,1:T(8,128)(2,1)S(1)}, bf16[512,768]{0,1:T(8,128)(2,1)}, u32[]{:S(2)}) copy-start(bf16[512,768]{0,1:T(8,128)(2,1)} %copy.105) | copy-start | bytes 2359300
  176.5 8.1 %copy-start.17 = (bf16[512,768]{0,1:T(8,128)(2,1)S(1)}, bf16[512,768]{0,1:T(8,128)(2,1)}, u32[]{:S(2)}) copy-start(bf16[512,768]{0,1:T(8,128)(2,1)} %copy.109) | copy-start | bytes 2359300
  176.5 8.1 %copy-start.31 = (f32[12,512]{1,0:T(8,128)S(1)}, f32[12,512]{1,0:T(8,128)}, u32[]{:S(2)}) copy-start(f32[12,512]{1,0:T(8,128)} %log_add_fusion.1) | copy-start | bytes 73732
  176.5 18.0 %slice-start.3 = ((s8[12582912]{0:T(1024)(128)(4,1)}), s8[4194304]{0:T(1024)(128)(4,1)S(1)}, s32[]{:S(2)}) async-start(s8[12582912]{0:T(1024)(128)(4,1)} %bitcast.203), calls=%async_computation.12 | async-start | bytes 8388608
  176.5 18.0 %slice-start.4 = ((s8[12582912]{0:T(1024)(128)(4,1)}), s8[4194304]{0:T(1024)(128)(4,1)S(1)}, s32[]{:S(2)}) async-start(s8[12582912]{0:T(1024)(128)(4,1)} %bitcast.203), calls=%async_computation.13 | async-start | bytes 8388608
  184.7 22.8 %copy-start.67 = (bf16[12,64,512]{2,1,0:T(8,128)(2,1)}, bf16[12,64,512]{2,1,0:T(8,128)(2,1)S(1)}, u32[]{:S(2)}) copy-start(bf16[12,64,512]{2,1,0:T(8,128)(2,1)S(1)} %fusion.62) | copy-start | bytes 2359300
  184.7 9.9 %slice-start.5 = ((s8[12582912]{0:T(1024)(128)(4,1)}), s8[4194304]{0:T(1024)(128)(4,1)S(1)}, s32[]{:S(2)}) async-start(s8[12582912]{0:T(1024)(128)(4,1)} %bitcast.203), calls=%async_computation.14 | async-start | bytes 8388608
  194.5 7.3 copy-start.6
  203.9 3.6 copy-start.27
  203.9 3.6 copy-start.13
  205.1 6.8 copy-start.18
  216.8 13.4 %all-to-all-start.8 = ((bf16[16,2,168]{2,1,0:T(2,128)(2,1)}), bf16[16,2,168]{2,1,0:T(2,128)(2,1)S(1)}, u32[]{:S(2)}, u32[]{:S(2)}) async-start(bf16[16,2,168]{2,1,0:T(2,128)(2,1)} %reshape.394), calls=%async_computation.8 | async-start | bytes 32768 | tf_op jit(solution)/shard_map/all_to_all | solution.py:316
  230.2 34.5 %all-to-all-start.4 = ((bf16[16,48,768]{2,1,0:T(8,128)(2,1)}), bf16[16,48,768]{2,1,0:T(8,128)(2,1)}, u32[]{:S(2)}, u32[]{:S(2)}) async-start(bf16[16,48,768]{2,1,0:T(8,128)(2,1)} %convolution_convert_fusion.7), calls=%async_computation.4 | async-start | bytes 2359296 | tf_op jit(solution)/shard_map/all_to_all | solution.py:288
  238.9 3.7 copy-start.59
  264.7 32.9 %all-to-all-start.2 = ((bf16[16,48,768]{2,1,0:T(8,128)(2,1)}), bf16[16,48,768]{2,1,0:T(8,128)(2,1)}, u32[]{:S(2)}, u32[]{:S(2)}) async-start(bf16[16,48,768]{2,1,0:T(8,128)(2,1)} %convolution_convert_fusion.8), calls=%async_computation.2 | async-start | bytes 2359296 | tf_op jit(solution)/shard_map/all_to_all | solution.py:274
  269.9 13.5 %slice-start = ((s8[12582912]{0:T(1024)(128)(4,1)}), s8[4194304]{0:T(1024)(128)(4,1)S(1)}, s32[]{:S(2)}) async-start(s8[12582912]{0:T(1024)(128)(4,1)} %bitcast.201), calls=%async_computation.9 | async-start | bytes 8388608
  269.9 13.5 %slice-start.1 = ((s8[12582912]{0:T(1024)(128)(4,1)}), s8[4194304]{0:T(1024)(128)(4,1)S(1)}, s32[]{:S(2)}) async-start(s8[12582912]{0:T(1024)(128)(4,1)} %bitcast.201), calls=%async_computation.10 | async-start | bytes 8388608
  269.9 13.5 %slice-start.2 = ((s8[12582912]{0:T(1024)(128)(4,1)}), s8[4194304]{0:T(1024)(128)(4,1)S(1)}, s32[]{:S(2)}) async-start(s8[12582912]{0:T(1024)(128)(4,1)} %bitcast.201), calls=%async_computation.11 | async-start | bytes 8388608
  270.0 13.5 %copy-start.8 = (pred[512,512]{0,1:T(8,128)(4,1)S(1)}, pred[512,512]{0,1:T(8,128)(4,1)}, u32[]{:S(2)}) copy-start(pred[512,512]{0,1:T(8,128)(4,1)} %get-tuple-element.52) | copy-start | bytes 786436
  270.0 13.5 %copy-start.29 = (f32[12,512]{1,0:T(8,128)S(1)}, f32[12,512]{1,0:T(8,128)}, u32[]{:S(2)}) copy-start(f32[12,512]{1,0:T(8,128)} %log_add_fusion) | copy-start | bytes 73732
  283.5 7.1 copy-start.4
  297.6 32.7 %all-to-all-start = ((bf16[16,48,768]{2,1,0:T(8,128)(2,1)}), bf16[16,48,768]{2,1,0:T(8,128)(2,1)}, u32[]{:S(2)}, u32[]{:S(2)}) async-start(bf16[16,48,768]{2,1,0:T(8,128)(2,1)} %bitcast.231), calls=%async_computation | async-start | bytes 2359296 | tf_op jit(solution)/shard_map/all_to_all | solution.py:260
  330.4 58.5 %all-to-all-start.7 = ((bf16[16,96,768]{2,1,0:T(8,128)(2,1)}), bf16[16,96,768]{2,1,0:T(8,128)(2,1)}, u32[]{:S(2)}, u32[]{:S(2)}) async-start(bf16[16,96,768]{2,1,0:T(8,128)(2,1)} %bitcast.229), calls=%async_computation.7 | async-start | bytes 4718592 | tf_op jit(solution)/shard_map/all_to_all | solution.py:309
  335.8 5.1 copy-start.9
  335.8 5.1 copy-start.16
  335.9 5.1 copy-start.30
  347.3 37.0 %copy-start.64 = (bf16[1,512,768]{2,1,0:T(8,128)(2,1)S(1)}, bf16[1,512,768]{2,1,0:T(8,128)(2,1)}, u32[]{:S(2)}) copy-start(bf16[1,512,768]{2,1,0:T(8,128)(2,1)} %param.15) | copy-start | bytes 2359300
  347.5 35.7 %collective-permute-start.3 = (bf16[512,1536]{0,1:T(8,128)(2,1)S(1)}, bf16[512,1536]{0,1:T(8,128)(2,1)S(1)}, u32[]{:S(2)}, u32[]{:S(2)}) collective-permute-start(bf16[512,1536]{0,1:T(8,128)(2,1)S(1)} %pad_maximum_fusion.2), channel_id=1, source_target_pairs={{0,16},{16,0},{1,17},{17,1},{2,18},{18,2},{3,19},{19,3},{4,20},{20... | collective-permute-start | bytes 4718600 | tf_op jit(solution)/shard_map/ppermute | solution.py:14
  388.8 58.4 %all-to-all-start.1 = ((bf16[16,48,1536]{2,1,0:T(8,128)(2,1)}), bf16[16,48,1536]{2,1,0:T(8,128)(2,1)}, u32[]{:S(2)}, u32[]{:S(2)}) async-start(bf16[16,48,1536]{2,1,0:T(8,128)(2,1)} %bitcast.230), calls=%async_computation.1 | async-start | bytes 4718592 | tf_op jit(solution)/shard_map/all_to_all | solution.py:267
  447.2 83.3 %all-to-all-start.3 = ((bf16[16,48,2304]{2,1,0:T(8,128)(2,1)}), bf16[16,48,2304]{2,1,0:T(8,128)(2,1)}, u32[]{:S(2)}, u32[]{:S(2)}) async-start(bf16[16,48,2304]{2,1,0:T(8,128)(2,1)} %bitcast.215), calls=%async_computation.3 | async-start | bytes 7077888 | tf_op jit(solution)/shard_map/all_to_all | solution.py:281
  530.6 108.8 %all-to-all-start.5 = ((bf16[16,48,3072]{2,1,0:T(8,128)(2,1)}), bf16[16,48,3072]{2,1,0:T(8,128)(2,1)}, u32[]{:S(2)}, u32[]{:S(2)}) async-start(bf16[16,48,3072]{2,1,0:T(8,128)(2,1)} %bitcast.214), calls=%async_computation.5 | async-start | bytes 9437184 | tf_op jit(solution)/shard_map/all_to_all | solution.py:295
  639.4 108.6 %all-to-all-start.6 = ((bf16[16,192,768]{2,1,0:T(8,128)(2,1)}), bf16[16,192,768]{2,1,0:T(8,128)(2,1)}, u32[]{:S(2)}, u32[]{:S(2)}) async-start(bf16[16,192,768]{2,1,0:T(8,128)(2,1)} %bitcast.213), calls=%async_computation.6 | async-start | bytes 9437184 | tf_op jit(solution)/shard_map/all_to_all | solution.py:302
  (29 other events, 55.0 us)
where the time goes:
time: 760 us; the launch traced here: 752 us
  waiting for transfers between devices  420 us (55%)
  matrix products  169 us (22%)
  other arithmetic  63.1 us (8%)
  starting transfers between devices  52.8 us (7%)
  local copies, waits for them, and re-layouts  44.5 us (6%)
    all_to_all x1, waiting for transfers between devices, body(): lax.all_to_all(owner_pieces(grad_ffn_in_w, doc_count).astype(jnp.bfloat16...  96.3 us
    ppermute x4, waiting for transfers between devices, from_partner(): lax.ppermute(shard, axis, [(i, i ^ 1 << distance) for i in range(lax.axis...  92.4 us
    all_to_all x1, waiting for transfers between devices, body(): lax.all_to_all(owner_pieces(grad_ffn_out_w, doc_count).astype(jnp.bfloat1...  72.2 us
    all_to_all x1, waiting for transfers between devices, body(): lax.all_to_all(owner_pieces(grad_self_qkv_w, doc_count).astype(jnp.bfloat...  70.9 us
    all_to_all x1, waiting for transfers between devices, body(): lax.all_to_all(owner_pieces(grad_cross_kv_w, doc_count).astype(jnp.bfloat...  47 us
    dot_general x8, matrix products, outer_sum(): lax.dot_general(left, right, (((0,), (0,)), ((), ())), preferred_element_...  37.2 us
    dot_general x8, matrix products, times_transposed(): lax.dot_general(left, right, (((1,), (1,)), ((), ())), preferred_element_...  33.1 us
    reduce_sum x9, other arithmetic, add_pieces(): return tuple((jnp.sum(piece, axis=0) for piece in received))  23.8 us
  transfers between devices with their start and end apart: 13, of which 13 were waited for; matrix products, arithmetic and copies ran while one was open for 16% of the time, Pallas kernels for 0%

commit v1 on v0

--- a/solution.py
+++ b/solution.py
@@ -36,20 +36,65 @@
     )
 
 
-def owner_pieces(term, doc_count):
-    return term.reshape((doc_count, term.shape[0] // doc_count) + term.shape[1:])
-
-
-def add_pieces(received):
-    return tuple((jnp.sum(piece, axis=0) for piece in received))
+def bit_of(index, bit):
+    return (index >> bit) & 1
+
+
+def take_half(stacked, axis, which):
+    return lax.dynamic_index_in_dim(stacked, which, axis, keepdims=False)
+
+
+def reduce_pair_columns(left, right):
+    index = lax.axis_index("docs")
+    core = bit_of(index, 0)
+    width = right.shape[1] // 2
+    sent = outer_sum(left, lax.dynamic_slice_in_dim(right, (1 - core) * width, width, 1))
+    received = from_partner(sent.astype(jnp.bfloat16), "docs", 0)
+    kept = outer_sum(left, lax.dynamic_slice_in_dim(right, core * width, width, 1))
+    return kept + received.astype(jnp.float32)
+
+
+def reduce_rows(half, bits):
+    doc_count = lax.axis_size("docs")
+    index = lax.axis_index("docs")
+    levels = doc_count.bit_length() - 1
+    names = list(range(levels - 1, 0, -1))
+    rows = half.shape[0] // doc_count
+    part = half.reshape((2,) * len(names) + (2 * rows, half.shape[1]))
+    for bit in bits:
+        axis = names.index(bit)
+        mine = bit_of(index, bit)
+        sent = take_half(part, axis, 1 - mine).astype(jnp.bfloat16)
+        received = from_partner(sent, "docs", bit)
+        part = take_half(part, axis, mine) + received.astype(jnp.float32)
+        names.pop(axis)
+    core = bit_of(index, 0)
+    part = part.reshape(2, rows, half.shape[1])
+    received = from_partner(take_half(part, 0, 1 - core).astype(jnp.bfloat16), "docs", 0)
+    own = take_half(part, 0, core)
+    other = received.astype(jnp.float32)
+    return jnp.concatenate(
+        [jnp.where(core == 0, own, other), jnp.where(core == 0, other, own)], axis=1
+    )
+
+
+def bit_order(first):
+    levels = lax.axis_size("docs").bit_length() - 1
+    near = list(range(1, levels))
+    return near if first == 0 else near[1:] + near[:1]
+
+
+def summed_gradient(left, right, first=0):
+    return reduce_rows(reduce_pair_columns(left, right), bit_order(first))
 
 
 def layout(text_row, visual_row, tokens):
-    doc_ends = jnp.cumsum(text_row)
+    order = jnp.arange(text_row.shape[0], dtype=jnp.int32)
+    doc_ends = jnp.sum(jnp.where(order[None, :] <= order[:, None], text_row[None, :], 0), axis=1)
     doc_starts = doc_ends - text_row
     positions = jnp.arange(tokens, dtype=jnp.int32)
     doc_ids = jnp.sum((positions[:, None] >= doc_ends[None, :]).astype(jnp.int32), axis=1)
-    member = doc_ids[:, None] == jnp.arange(text_row.shape[0], dtype=jnp.int32)[None, :]
+    member = doc_ids[:, None] == order[None, :]
     row_start = jnp.sum(jnp.where(member, doc_starts[None, :], 0), axis=1)
     row_visual = jnp.sum(jnp.where(member, visual_row[None, :], 0), axis=1)
     visible = positions - row_start < row_visual
@@ -81,45 +126,42 @@
     results = jnp.einsum(
         "hqk,khd->qhd", attn_probs, value_heads, preferred_element_type=jnp.float32
     )
-    log_sums = [row_max + jnp.log(row_total)]
-    return (results.reshape(tokens, -1), log_sums)
+    return (results.reshape(tokens, -1), row_max + jnp.log(row_total))
 
 
 def attend_back(queries, key_rows, value_rows, out_grad, log_sums, doc_ids, key_valid):
     tokens = queries.shape[0]
-    block_rows = min(512, tokens)
     query_heads = split_heads(queries)
     key_heads = split_heads(key_rows)
     value_heads = split_heads(value_rows)
     out_heads = split_heads(out_grad)
     score_scale = HD ** (-0.5)
-    query_grads = []
-    key_grad = jnp.zeros(key_heads.shape, jnp.float32)
-    value_grad = jnp.zeros(value_heads.shape, jnp.float32)
-    for block_index, row_start in enumerate(range(0, tokens, block_rows)):
-        scores = block_scores(query_heads, key_heads, doc_ids, key_valid)
-        attn_probs = jnp.exp(scores - log_sums[block_index])
-        prob_grad = jnp.einsum(
-            "qhd,khd->hqk", out_heads, value_heads, preferred_element_type=jnp.float32
-        )
-        inner = jnp.sum(attn_probs * prob_grad, axis=-1, keepdims=True)
-        score_grad = (attn_probs * (prob_grad - inner)).astype(jnp.bfloat16)
-        query_grads.append(
-            jnp.einsum("hqk,khd->qhd", score_grad, key_heads, preferred_element_type=jnp.float32)
-            * score_scale
-        )
-        key_grad = (
-            jnp.einsum("hqk,qhd->khd", score_grad, query_heads, preferred_element_type=jnp.float32)
-            * score_scale
-        )
-        value_grad = jnp.einsum(
-            "hqk,qhd->khd",
-            attn_probs.astype(jnp.bfloat16),
-            out_heads,
-            preferred_element_type=jnp.float32,
-        )
-    query_grad = query_grads[0].reshape(tokens, -1)
-    return (query_grad, key_grad.reshape(tokens, -1), value_grad.reshape(tokens, -1))
+    scores = block_scores(query_heads, key_heads, doc_ids, key_valid)
+    attn_probs = jnp.exp(scores - log_sums)
+    prob_grad = jnp.einsum(
+        "qhd,khd->hqk", out_heads, value_heads, preferred_element_type=jnp.float32
+    )
+    inner = jnp.sum(attn_probs * prob_grad, axis=-1, keepdims=True)
+    score_grad = (attn_probs * (prob_grad - inner)).astype(jnp.bfloat16)
+    query_grad = (
+        jnp.einsum("hqk,khd->qhd", score_grad, key_heads, preferred_element_type=jnp.float32)
+        * score_scale
+    )
+    key_grad = (
+        jnp.einsum("hqk,qhd->khd", score_grad, query_heads, preferred_element_type=jnp.float32)
+        * score_scale
+    )
+    value_grad = jnp.einsum(
+        "hqk,qhd->khd",
+        attn_probs.astype(jnp.bfloat16),
+        out_heads,
+        preferred_element_type=jnp.float32,
+    )
+    return (
+        query_grad.reshape(tokens, -1),
+        key_grad.reshape(tokens, -1),
+        value_grad.reshape(tokens, -1),
+    )
 
 
 def body(
@@ -143,7 +185,6 @@
     cot_rows = cotangent[0].astype(jnp.float32)
     tokens = features.shape[0]
     model_width = features.shape[1]
-    doc_count = lax.axis_size("docs")
     half_index = lax.axis_index("stream")
     doc_ids, visible = layout(text_counts[0], visual_counts[0], tokens)
     visible_float = visible.astype(jnp.float32)
@@ -204,7 +245,7 @@
     logit_grad = gate_grad * gate_value * (1.0 - gate_value)
     grad_gate_shift = jnp.sum(logit_grad, axis=0)
     logit_low = logit_grad.astype(jnp.bfloat16)
-    grad_gate_w = outer_sum(gate_in, logit_low)
+    summed_gate_w = summed_gradient(gate_in, logit_low)
     gate_in_grad = times_transposed(logit_low, gate_w)
     partner_grad = gate_in_grad[:, model_width:] + out_grad * (1.0 - gate_value)
     returned_third = from_partner(partner_grad.astype(jnp.bfloat16), "stream", 0)
@@ -213,31 +254,30 @@
     ) * own_valid[:, None]
     third_in_grad, gain_grad_c, shift_grad_c = third_pull(third_grad)
     third_in_low = third_in_grad.astype(jnp.bfloat16)
-    grad_ffn_out_w = outer_sum(hidden, third_in_low)
+    summed_ffn_out = summed_gradient(hidden, third_in_low)
     hidden_grad = times_transposed(third_in_low, ffn_out)
     (pre_grad,) = gelu_pull(hidden_grad)
     pre_low = pre_grad.astype(jnp.bfloat16)
-    grad_ffn_in_w = outer_sum(second_low, pre_low)
+    summed_ffn_in = summed_gradient(second_low, pre_low)
     second_grad = third_in_grad + times_transposed(pre_low, ffn_in)
     second_in_grad, gain_grad_b, shift_grad_b = second_pull(second_grad)
     second_in_low = second_in_grad.astype(jnp.bfloat16)
-    grad_self_out_w = outer_sum(self_low, second_in_low)
+    summed_self_out = summed_gradient(self_low, second_in_low, 1)
     self_res_grad = times_transposed(second_in_low, self_out_w).astype(jnp.bfloat16)
     self_q_grad, self_k_grad, self_v_grad = attend_back(
         self_queries, self_keys, self_values, self_res_grad, self_sums, doc_ids, own_keys
     )
     qkv_low = jnp.concatenate([self_q_grad, self_k_grad, self_v_grad], axis=1).astype(jnp.bfloat16)
-    grad_self_qkv_w = outer_sum(first_low, qkv_low)
+    summed_self_qkv = summed_gradient(first_low, qkv_low, 1)
     first_grad = second_in_grad + times_transposed(qkv_low, self_qkv_w)
     first_in_grad, gain_grad_a, shift_grad_a = first_pull(first_grad)
     first_in_low = first_in_grad.astype(jnp.bfloat16)
-    grad_cross_out_w = outer_sum(cross_low, first_in_low)
+    summed_cross_out = summed_gradient(cross_low, first_in_low)
     cross_res_grad = times_transposed(first_in_low, cross_out).astype(jnp.bfloat16)
-    partner_again = from_partner(own_kv, "stream", 0)
     cross_q_grad, partner_k_grad, partner_v_grad = attend_back(
         queries,
-        partner_again[:, :model_width],
-        partner_again[:, model_width:],
+        partner_kv[:, :model_width],
+        partner_kv[:, model_width:],
         cross_res_grad,
         cross_sums,
         doc_ids,
@@ -246,8 +286,8 @@
     partner_kv_grad = jnp.concatenate([partner_k_grad, partner_v_grad], axis=1).astype(jnp.bfloat16)
     returned_kv = from_partner(partner_kv_grad, "stream", 0)
     cross_q_low = cross_q_grad.astype(jnp.bfloat16)
-    grad_cross_q_w = outer_sum(features, cross_q_low)
-    grad_cross_kv_w = outer_sum(features, returned_kv)
+    summed_cross_q = summed_gradient(features, cross_q_low)
+    summed_cross_kv = summed_gradient(features, returned_kv)
     feature_grad = (
         first_in_grad
         + times_transposed(cross_q_low, cross_q)
@@ -255,87 +295,14 @@
     )
     gain_grads = jnp.stack([gain_grad_a, gain_grad_b, gain_grad_c])
     shift_grads = jnp.stack([shift_grad_a, shift_grad_b, shift_grad_c])
-    small_cols = jnp.concatenate([gain_grads, shift_grads, grad_gate_shift[None]], axis=0).T
-    all_parts = (
-        lax.all_to_all(
-            owner_pieces(grad_cross_q_w, doc_count).astype(jnp.bfloat16),
-            "docs",
-            split_axis=0,
-            concat_axis=0,
-            tiled=True,
-        ).astype(jnp.float32),
-        lax.all_to_all(
-            owner_pieces(grad_cross_kv_w, doc_count).astype(jnp.bfloat16),
-            "docs",
-            split_axis=0,
-            concat_axis=0,
-            tiled=True,
-        ).astype(jnp.float32),
-        lax.all_to_all(
-            owner_pieces(grad_cross_out_w, doc_count).astype(jnp.bfloat16),
-            "docs",
-            split_axis=0,
-            concat_axis=0,
-            tiled=True,
-        ).astype(jnp.float32),
-        lax.all_to_all(
-            owner_pieces(grad_self_qkv_w, doc_count).astype(jnp.bfloat16),
-            "docs",
-            split_axis=0,
-            concat_axis=0,
-            tiled=True,
-        ).astype(jnp.float32),
-        lax.all_to_all(
-            owner_pieces(grad_self_out_w, doc_count).astype(jnp.bfloat16),
-            "docs",
-            split_axis=0,
-            concat_axis=0,
-            tiled=True,
-        ).astype(jnp.float32),
-        lax.all_to_all(
-            owner_pieces(grad_ffn_in_w, doc_count).astype(jnp.bfloat16),
-            "docs",
-            split_axis=0,
-            concat_axis=0,
-            tiled=True,
-        ).astype(jnp.float32),
-        lax.all_to_all(
-            owner_pieces(grad_ffn_out_w, doc_count).astype(jnp.bfloat16),
-            "docs",
-            split_axis=0,
-            concat_axis=0,
-            tiled=True,
-        ).astype(jnp.float32),
-        lax.all_to_all(
-            owner_pieces(grad_gate_w, doc_count).astype(jnp.bfloat16),
-            "docs",
-            split_axis=0,
-            concat_axis=0,
-            tiled=True,
-        ).astype(jnp.float32),
-        lax.all_to_all(
-            owner_pieces(small_cols, doc_count).astype(jnp.bfloat16),
-            "docs",
-            split_axis=0,
-            concat_axis=0,
-            tiled=True,
-        ).astype(jnp.float32),
-    )
-    (
-        summed_cross_q,
-        summed_cross_kv,
-        summed_cross_out,
-        summed_self_qkv,
-        summed_self_out,
-        summed_ffn_in,
-        summed_ffn_out,
-        summed_gate_w,
-        summed_small,
-    ) = add_pieces(all_parts)
-    summed_rows = summed_small.T
-    summed_gains = summed_rows[0:3]
-    summed_shifts = summed_rows[3:6]
-    summed_gate_shift = summed_rows[6]
+    small_rows = jnp.concatenate([gain_grads, shift_grads, grad_gate_shift[None]], axis=0)
+    gathered = lax.all_gather(small_rows, "docs")
+    summed_rows = lax.dynamic_slice_in_dim(
+        jnp.sum(gathered, axis=0),
+        lax.axis_index("docs") * (model_width // lax.axis_size("docs")),
+        model_width // lax.axis_size("docs"),
+        1,
+    )
     return (
         combined[None],
         feature_grad[None],
@@ -347,9 +314,9 @@
         summed_ffn_in[None],
         summed_ffn_out[None],
         summed_gate_w[None],
-        summed_gains[None],
-        summed_shifts[None],
-        summed_gate_shift[None],
+        summed_rows[None, 0:3],
+        summed_rows[None, 3:6],
+        summed_rows[None, 6],
     )
 
 

time: 760 us -> 575 us (0.76)
  the two profiles are of different devices: /device:TPU:15 before, /device:TPU:0 now
where the time goes in v1:
time: 575 us; the launch traced here: 567 us
  waiting for transfers between devices  240 us (42%)
  matrix products  157 us (27%)
  other arithmetic  58.7 us (10%)
  local copies, waits for them, and re-layouts  51 us (9%)
  starting transfers between devices  32.9 us (6%)
  blocking collectives  23.9 us (4%)
    ppermute x44, waiting for transfers between devices, from_partner(): lax.ppermute(shard, axis, [(i, i ^ 1 << distance) for i in range(lax.axis...  240 us
    ppermute x44, starting transfers between devices, from_partner(): lax.ppermute(shard, axis, [(i, i ^ 1 << distance) for i in range(lax.axis...  32.9 us
    dot_general x16, matrix products, outer_sum(): lax.dot_general(left, right, (((0,), (0,)), ((), ())), preferred_element_...  32.3 us
    dot_general x8, matrix products, times_transposed(): lax.dot_general(left, right, (((1,), (1,)), ((), ())), preferred_element_...  29.1 us
    all_gather x1, blocking collectives, body(): gathered = lax.all_gather(small_rows, 'docs')  23.9 us
    dot_general x2, matrix products, attend_back(): jnp.einsum('qhd,khd->hqk', out_heads, value_heads, preferred_element_type...  20.7 us
    dot_general x1, matrix products, body(): pre_act = jnp.dot(second_low, ffn_in, preferred_element_type=jnp.float32)  19.3 us
    dot_general x2, matrix products, attend_back(): jnp.einsum('hqk,qhd->khd', attn_probs.astype(jnp.bfloat16), out_heads, pr...  16.2 us
  transfers between devices with their start and end apart: 44, of which 27 were waited for; matrix products, arithmetic and copies ran while one was open for 31% of the time, Pallas kernels for 0%

profile of v1, /device:TPU:0, one launch (start us, length us, event | category | flops | bytes accessed | tf_op | source)
XLA Modules:
  0.0 567.1 jit_solution(117856154041441380)
XLA Ops:
  0.7 4.6 convolution_convert_fusion.4
  5.2 3.0 collective-permute-start
  10.2 3.2 convolution_convert_fusion.9
  13.4 2.3 copy.91
  20.0 22.9 %collective-permute-done = bf16[512,1536]{1,0:T(8,128)(2,1)} collective-permute-done((bf16[512,1536]{1,0:T(8,128)(2,1)}, bf16[512,1536]{1,0:T(8,128)(2,1)}, u32[]{:S(2)}, u32[]{:S(2)}) %collective-permute-start) | collective-permute-done | bytes 1572896 | tf_op jit(solution)/shard_map/ppermute | solution.py:14
  42.9 2.6 fusion.195
  47.8 2.3 copy.90
  50.1 3.5 fusion.26
  53.7 3.7 fusion
  58.4 5.3 fusion.75
  69.7 2.3 copy.96
  72.0 2.3 copy.95
  74.3 2.3 copy.94
  76.6 3.5 fusion.27
  80.2 3.7 fusion.1
  84.9 5.1 fusion.74
  92.3 19.3 %multiply_convert_fusion.2 = (bf16[512,3072]{1,0:T(8,128)(2,1)S(1)}, f32[512,3072]{1,0:T(8,128)}, f32[512,3072]{1,0:T(8,128)}) fusion(bf16[1,768,3072]{2,1,0:T(8,128)(2,1)} %param.24, f32[512,768]{1,0:T(8,128)S(1)} %get-tuple-element.76, f32[768]{0:T(1024)S(1)} %copy-done.106, f32[768]{0:T(1024)S(1)} %copy-done.94, f32[512]{0:T(512)S(1)} %fusion.171, ...), kind=kOutput, calls=%fused_computation.23 | convolution fusion | flops 2520121344 | bytes 22030336 | tf_op jit(solution)/shard_map/dot_general | solution.py:229
  111.6 2.8 fusion.199
  117.0 16.9 %collective-permute-done.1 = bf16[512,768]{1,0:T(8,128)(2,1)S(1)} collective-permute-done((bf16[512,768]{1,0:T(8,128)(2,1)S(1)}, bf16[512,768]{1,0:T(8,128)(2,1)S(1)}, u32[]{:S(2)}, u32[]{:S(2)}) %collective-permute-start.1) | collective-permute-done | bytes 786464 | tf_op jit(solution)/shard_map/ppermute | solution.py:14
  135.6 3.0 fusion.187
  147.4 3.7 convolution_convert_fusion.5
  151.0 9.0 %collective-permute-done.2 = bf16[512,768]{1,0:T(8,128)(2,1)} collective-permute-done((bf16[512,768]{1,0:T(8,128)(2,1)}, bf16[512,768]{1,0:T(8,128)(2,1)}, u32[]{:S(2)}, u32[]{:S(2)}) %collective-permute-start.2) | collective-permute-done | bytes 786464 | tf_op jit(solution)/shard_map/ppermute | solution.py:14
  160.0 3.2 multiply_reduce_fusion.2
  164.1 9.5 %add_convert_fusion = bf16[512,3072]{1,0:T(8,128)(2,1)} fusion(f32[512,3072]{1,0:T(8,128)} %get-tuple-element.40, f32[512,3072]{1,0:T(8,128)} %get-tuple-element.77, bf16[512,768]{1,0:T(8,128)(2,1)S(1)} %add_convert_fusion.3, bf16[1,3072,768]{2,1,0:T(8,128)(2,1)S(1)} %bitcast.423), kind=kOutput, calls=%fused_computation.22 | convolution fusion | flops 2437939200 | bytes 21233664 | tf_op jit(solution)/shard_map/dot_general | solution.py:28
  173.7 5.6 multiply_reduce_fusion.3
  184.8 3.3 convolution_convert_fusion.1
  188.1 2.3 copy.98
  190.5 8.1 %fusion.68 = bf16[12,64,512]{2,1,0:T(8,128)(2,1)S(1)} fusion(bf16[512,12,64]{0,2,1:T(8,128)(2,1)} %bitcast.382, f32[12,512]{1,0:T(8,128)} %log_add_fusion.1, f32[12,512,512]{1,2,0:T(8,128)} %copy-done.2, pred[512,512]{0,1:T(8,128)(4,1)} %get-tuple-element.67), kind=kOutput, calls=%fused_computation.133 | convolution fusion | flops 415629312 | bytes 14442496 | tf_op jit(solution)/shard_map/hqk,qhd->khd/dot_general | solution.py:154
  198.6 9.7 %multiply_reduce_fusion.1 = (f32[12,512]{1,0:T(8,128)S(1)}, f32[12,512,512]{1,2,0:T(8,128)}) fusion(f32[12,512]{1,0:T(8,128)S(1)} %copy-done.72, f32[12,512,512]{1,2,0:T(8,128)} %copy-done.2, pred[512,512]{0,1:T(8,128)(4,1)S(1)} %copy-done.20, bf16[512,12,64]{0,2,1:T(8,128)(2,1)S(1)} %bitcast.383, bf16[512,12,64]{0,2,1:T(8,128)(2,1)S(1)} %bitcast.381), kind=kOutput, calls=%fused_computation.4 | convolution fusion | flops 418375680 | bytes 27049984 | tf_op jit(solution)/shard_map/qhd,khd->hqk/dot_general | solution.py:141
  208.3 7.2 %multiply_convert_fusion.1 = bf16[12,512,512]{1,2,0:T(8,128)(2,1)S(1)} fusion(f32[12,512,512]{1,2,0:T(8,128)} %get-tuple-element.82, f32[12,512]{1,0:T(8,128)S(1)} %get-tuple-element.81, f32[12,512]{1,0:T(8,128)S(1)} %copy-done.72, f32[12,512,512]{1,2,0:T(8,128)S(1)} %bitcast.352, pred[512,512]{0,1:T(8,128)(4,1)S(1)} %copy-done.20), kind=kLoop, calls=%fused_computation.3 | loop fusion | flops 18874368 | bytes 31768576 | tf_op jit(solution)/shard_map/convert_element_type | solution.py:145
  219.5 4.4 multiply_reduce_fusion.4
  230.3 23.9 %all-gather.1 = f32[16,7,768]{2,1,0:T(8,128)} all-gather(f32[1,7,768]{2,1,0:T(8,128)} %bitcast.418), channel_id=2, replica_groups=mesh['stream'=2,'docs'=16] {'docs'}, dimensions={0}, use_global_device_ids=true | all-gather | bytes 365568 | tf_op jit(solution)/shard_map/all_gather | solution.py:299
  258.4 2.5 fusion.189
  265.7 2.3 copy.102
  268.0 8.1 %fusion.71 = bf16[12,64,512]{2,1,0:T(8,128)(2,1)S(1)} fusion(bf16[512,12,64]{0,2,1:T(8,128)(2,1)} %bitcast.384, f32[12,512]{1,0:T(8,128)} %log_add_fusion, f32[12,512,512]{1,2,0:T(8,128)} %copy-done.1, pred[512,512]{0,1:T(8,128)(4,1)} %get-tuple-element.68), kind=kOutput, calls=%fused_computation.134 | convolution fusion | flops 415629312 | bytes 14442496 | tf_op jit(solution)/shard_map/hqk,qhd->khd/dot_general | solution.py:154
  276.2 11.0 %multiply_reduce_fusion = (f32[12,512]{1,0:T(8,128)S(1)}, f32[12,512,512]{1,2,0:T(8,128)}) fusion(f32[12,512]{1,0:T(8,128)S(1)} %copy-done.71, f32[12,512,512]{1,2,0:T(8,128)} %copy-done.1, pred[512,512]{0,1:T(8,128)(4,1)S(1)} %copy-done.19, bf16[512,12,64]{0,2,1:T(8,128)(2,1)S(1)} %bitcast.385, bf16[512,12,64]{0,2,1:T(8,128)(2,1)S(1)} %bitcast.379), kind=kOutput, calls=%fused_computation.1 | convolution fusion | flops 418375680 | bytes 27049984 | tf_op jit(solution)/shard_map/qhd,khd->hqk/dot_general | solution.py:141
  287.7 3.1 convolution_convert_fusion.2
  292.6 7.5 %multiply_convert_fusion = bf16[12,512,512]{1,2,0:T(8,128)(2,1)S(1)} fusion(f32[12,512,512]{1,2,0:T(8,128)} %get-tuple-element.85, f32[12,512]{1,0:T(8,128)S(1)} %get-tuple-element.84, f32[12,512]{1,0:T(8,128)S(1)} %copy-done.71, f32[12,512,512]{1,2,0:T(8,128)S(1)} %bitcast.350, pred[512,512]{0,1:T(8,128)(4,1)S(1)} %copy-done.19), kind=kLoop, calls=%fused_computation | loop fusion | flops 18874368 | bytes 31768576 | tf_op jit(solution)/shard_map/convert_element_type | solution.py:145
  302.1 2.5 convolution_convert_fusion.3
  310.2 2.3 convolution_add_fusion
  320.0 2.6 copy.106
  330.0 16.9 %collective-permute-done.5 = bf16[2,2,96,384]{3,2,1,0:T(8,128)(2,1)S(1)} collective-permute-done((bf16[2,2,96,384]{3,2,1,0:T(8,128)(2,1)S(1)}, bf16[2,2,96,384]{3,2,1,0:T(8,128)(2,1)S(1)}, u32[]{:S(2)}, u32[]{:S(2)}) %collective-permute-start.5) | collective-permute-done | bytes 294944 | tf_op jit(solution)/shard_map/ppermute | solution.py:14
  348.9 6.1 %collective-permute-done.16 = bf16[2,96,384]{2,1,0:T(8,128)(2,1)S(1)} collective-permute-done((bf16[2,96,384]{2,1,0:T(8,128)(2,1)S(1)}, bf16[2,96,384]{2,1,0:T(8,128)(2,1)S(1)}, u32[]{:S(2)}, u32[]{:S(2)}) %collective-permute-start.16) | collective-permute-done | bytes 147488 | tf_op jit(solution)/shard_map/ppermute | solution.py:14
  357.3 4.5 collective-permute-done.6
  362.0 4.2 collective-permute-done.27
  366.2 2.7 collective-permute-start.17
  368.9 4.2 collective-permute-done.17
  374.2 5.0 collective-permute-done.7
  386.1 8.0 %collective-permute-done.42 = bf16[192,384]{1,0:T(8,128)(2,1)S(1)} collective-permute-done((bf16[192,384]{1,0:T(8,128)(2,1)S(1)}, bf16[192,384]{1,0:T(8,128)(2,1)S(1)}, u32[]{:S(2)}, u32[]{:S(2)}) %collective-permute-start.42) | collective-permute-done | bytes 147488 | tf_op jit(solution)/shard_map/ppermute | solution.py:14
  396.3 23.0 %collective-permute-done.3 = bf16[512,1536]{0,1:T(8,128)(2,1)S(1)} collective-permute-done((bf16[512,1536]{0,1:T(8,128)(2,1)S(1)}, bf16[512,1536]{0,1:T(8,128)(2,1)S(1)}, u32[]{:S(2)}, u32[]{:S(2)}) %collective-permute-start.3) | collective-permute-done | bytes 1572896 | tf_op jit(solution)/shard_map/ppermute | solution.py:14
  420.3 2.9 convert_add_fusion.2
  423.8 2.7 add_bitcast_fusion
  426.6 3.6 convert_add_fusion
  430.4 15.4 %collective-permute-done.20 = bf16[2,2,96,1152]{3,2,1,0:T(8,128)(2,1)S(1)} collective-permute-done((bf16[2,2,96,1152]{3,2,1,0:T(8,128)(2,1)S(1)}, bf16[2,2,96,1152]{3,2,1,0:T(8,128)(2,1)S(1)}, u32[]{:S(2)}, u32[]{:S(2)}) %collective-permute-start.20) | collective-permute-done | bytes 884768 | tf_op jit(solution)/shard_map/ppermute | solution.py:14
  447.4 3.4 convert_add_fusion.1
  451.0 17.2 %collective-permute-done.21 = bf16[2,96,1152]{2,1,0:T(8,128)(2,1)S(1)} collective-permute-done((bf16[2,96,1152]{2,1,0:T(8,128)(2,1)S(1)}, bf16[2,96,1152]{2,1,0:T(8,128)(2,1)S(1)}, u32[]{:S(2)}, u32[]{:S(2)}) %collective-permute-start.21) | collective-permute-done | bytes 442400 | tf_op jit(solution)/shard_map/ppermute | solution.py:14
  471.4 17.7 %collective-permute-done.22 = bf16[96,1152]{1,0:T(8,128)(2,1)S(1)} collective-permute-done((bf16[96,1152]{1,0:T(8,128)(2,1)S(1)}, bf16[96,1152]{1,0:T(8,128)(2,1)S(1)}, u32[]{:S(2)}, u32[]{:S(2)}) %collective-permute-start.22) | collective-permute-done | bytes 221216 | tf_op jit(solution)/shard_map/ppermute | solution.py:14
  489.3 12.1 %collective-permute-done.10 = bf16[2,2,96,768]{3,2,1,0:T(8,128)(2,1)S(1)} collective-permute-done((bf16[2,2,96,768]{3,2,1,0:T(8,128)(2,1)S(1)}, bf16[2,2,96,768]{3,2,1,0:T(8,128)(2,1)S(1)}, u32[]{:S(2)}, u32[]{:S(2)}) %collective-permute-start.10) | collective-permute-done | bytes 589856 | tf_op jit(solution)/shard_map/ppermute | solution.py:14
  504.8 6.7 %collective-permute-done.11 = bf16[2,96,768]{2,1,0:T(8,128)(2,1)S(1)} collective-permute-done((bf16[2,96,768]{2,1,0:T(8,128)(2,1)S(1)}, bf16[2,96,768]{2,1,0:T(8,128)(2,1)S(1)}, u32[]{:S(2)}, u32[]{:S(2)}) %collective-permute-start.11) | collective-permute-done | bytes 294944 | tf_op jit(solution)/shard_map/ppermute | solution.py:14
  511.6 2.8 collective-permute-start.12
  514.8 10.3 %collective-permute-done.12 = bf16[96,768]{1,0:T(8,128)(2,1)S(1)} collective-permute-done((bf16[96,768]{1,0:T(8,128)(2,1)S(1)}, bf16[96,768]{1,0:T(8,128)(2,1)S(1)}, u32[]{:S(2)}, u32[]{:S(2)}) %collective-permute-start.12) | collective-permute-done | bytes 147488 | tf_op jit(solution)/shard_map/ppermute | solution.py:14
  525.3 3.6 collective-permute-start.31
  530.9 18.3 %collective-permute-done.31 = bf16[2,96,1536]{2,1,0:T(8,128)(2,1)S(1)} collective-permute-done((bf16[2,96,1536]{2,1,0:T(8,128)(2,1)S(1)}, bf16[2,96,1536]{2,1,0:T(8,128)(2,1)S(1)}, u32[]{:S(2)}, u32[]{:S(2)}) %collective-permute-start.31) | collective-permute-done | bytes 589856 | tf_op jit(solution)/shard_map/ppermute | solution.py:14
  549.6 14.8 %collective-permute-done.32 = bf16[96,1536]{1,0:T(8,128)(2,1)S(1)} collective-permute-done((bf16[96,1536]{1,0:T(8,128)(2,1)S(1)}, bf16[96,1536]{1,0:T(8,128)(2,1)S(1)}, u32[]{:S(2)}, u32[]{:S(2)}) %collective-permute-start.32) | collective-permute-done | bytes 294944 | tf_op jit(solution)/shard_map/ppermute | solution.py:14
  (483 shorter events, 111.4 us)
Async XLA Ops:
  0.6 65.5 %copy-start = (bf16[1,768,2304]{2,1,0:T(8,128)(2,1)S(1)}, bf16[1,768,2304]{2,1,0:T(8,128)(2,1)}, u32[]{:S(2)}) copy-start(bf16[1,768,2304]{2,1,0:T(8,128)(2,1)} %param.22) | copy-start | bytes 10616836
  5.2 37.7 %collective-permute-start = (bf16[512,1536]{1,0:T(8,128)(2,1)}, bf16[512,1536]{1,0:T(8,128)(2,1)}, u32[]{:S(2)}, u32[]{:S(2)}) collective-permute-start(bf16[512,1536]{1,0:T(8,128)(2,1)} %convolution_convert_fusion.4), channel_id=1, source_target_pairs={{0,16},{16,0},{1,17},{17,1},{2,18},{18,2},{3,19},{19,3},{4,20},{20... | collective-permute-start | bytes 4718600 | tf_op jit(solution)/shard_map/ppermute | solution.py:14
  64.7 25.3 %copy-start.78 = (f32[512]{0:T(512)}, f32[512]{0:T(512)S(1)}, u32[]{:S(2)}) copy-start(f32[512]{0:T(512)S(1)} %broadcast_multiply_fusion.2) | copy-start | bytes 6148
  90.1 21.5 %slice-start.6 = ((s8[4718592]{0:T(1024)(128)(4,1)}), s8[524288]{0:T(1024)(128)(4,1)S(1)}, s32[]{:S(2)}) async-start(s8[4718592]{0:T(1024)(128)(4,1)} %bitcast.420), calls=%async_computation.6 | async-start | bytes 1048576
  91.1 20.4 %copy-start.21 = (f32[512,768]{1,0:T(8,128)}, f32[512,768]{1,0:T(8,128)S(1)}, u32[]{:S(2)}) copy-start(f32[512,768]{1,0:T(8,128)S(1)} %get-tuple-element.76) | copy-start | bytes 4718596
  91.2 20.4 %copy-start.80 = (f32[512]{0:T(512)}, f32[512]{0:T(512)S(1)}, u32[]{:S(2)}) copy-start(f32[512]{0:T(512)S(1)} %broadcast_multiply_fusion.1) | copy-start | bytes 6148
  91.5 20.1 %copy-start.97 = (f32[512]{0:T(512)}, f32[512]{0:T(512)S(1)}, u32[]{:S(2)}) copy-start(f32[512]{0:T(512)S(1)} %fusion.171) | copy-start | bytes 6148
  92.3 19.3 %slice-start.7 = ((s8[4718592]{0:T(1024)(128)(4,1)}), s8[4194304]{0:T(1024)(128)(4,1)S(1)}, s32[]{:S(2)}) async-start(s8[4718592]{0:T(1024)(128)(4,1)} %bitcast.420), calls=%async_computation.7 | async-start | bytes 8388608
  114.4 21.1 %copy-start.3 = (f32[512,768]{1,0:T(8,128)}, f32[512,768]{1,0:T(8,128)S(1)}, u32[]{:S(2)}) copy-start(f32[512,768]{1,0:T(8,128)S(1)} %get-tuple-element.79) | copy-start | bytes 4718596
  114.4 19.6 %copy-start.111 = (bf16[1,1536,768]{2,1,0:T(8,128)(2,1)S(1)}, bf16[1,1536,768]{2,1,0:T(8,128)(2,1)}, u32[]{:S(2)}) copy-start(bf16[1,1536,768]{2,1,0:T(8,128)(2,1)} %param.26) | copy-start | bytes 7077892
  115.2 18.8 %copy-start.61 = (bf16[512,768]{1,0:T(8,128)(2,1)}, bf16[512,768]{1,0:T(8,128)(2,1)S(1)}, u32[]{:S(2)}) copy-start(bf16[512,768]{1,0:T(8,128)(2,1)S(1)} %fusion.186) | copy-start | bytes 2359300
  115.2 18.8 %collective-permute-start.1 = (bf16[512,768]{1,0:T(8,128)(2,1)S(1)}, bf16[512,768]{1,0:T(8,128)(2,1)S(1)}, u32[]{:S(2)}, u32[]{:S(2)}) collective-permute-start(bf16[512,768]{1,0:T(8,128)(2,1)S(1)} %fusion.186), channel_id=1, source_target_pairs={{0,16},{16,0},{1,17},{17,1},{2,18},{18,2},{3,19},{19,3},{4,20},{20... | collective-permute-start | bytes 2359304 | tf_op jit(solution)/shard_map/ppermute | solution.py:14
  117.0 18.5 %copy-start.14 = (bf16[1,512,768]{2,1,0:T(8,128)(2,1)S(1)}, bf16[1,512,768]{2,1,0:T(8,128)(2,1)}, u32[]{:S(2)}) copy-start(bf16[1,512,768]{2,1,0:T(8,128)(2,1)} %param.16) | copy-start | bytes 2359300
  141.9 18.1 %collective-permute-start.2 = (bf16[512,768]{1,0:T(8,128)(2,1)}, bf16[512,768]{1,0:T(8,128)(2,1)}, u32[]{:S(2)}, u32[]{:S(2)}) collective-permute-start(bf16[512,768]{1,0:T(8,128)(2,1)} %fusion.46), channel_id=1, source_target_pairs={{0,16},{16,0},{1,17},{17,1},{2,18},{18,2},{3,19},{19,3},{4,20},{20... | collective-permute-start | bytes 2359304 | tf_op jit(solution)/shard_map/ppermute | solution.py:14
  151.0 158.7 %collective-permute-start.39 = (bf16[1536,384]{1,0:T(8,128)(2,1)}, bf16[1536,384]{1,0:T(8,128)(2,1)}, u32[]{:S(2)}, u32[]{:S(2)}) collective-permute-start(bf16[1536,384]{1,0:T(8,128)(2,1)} %convolution_convert_fusion.5), channel_id=1, source_target_pairs={{0,1},{1,0},{2,3},{3,2},{4,5},{5,4},{6,7},{7,6},{8,9},{9,8},{10,11... | collective-permute-start | bytes 3538952 | tf_op jit(solution)/shard_map/ppermute | solution.py:14
  164.0 20.8 %copy-start.56 = (bf16[512,768]{1,0:T(8,128)(2,1)}, bf16[512,768]{1,0:T(8,128)(2,1)S(1)}, u32[]{:S(2)}) copy-start(bf16[512,768]{1,0:T(8,128)(2,1)S(1)} %add_convert_fusion.3) | copy-start | bytes 2359300
  190.5 17.8 %slice-start.3 = ((s8[12582912]{0:T(1024)(128)(4,1)}), s8[4194304]{0:T(1024)(128)(4,1)S(1)}, s32[]{:S(2)}) async-start(s8[12582912]{0:T(1024)(128)(4,1)} %bitcast.351), calls=%async_computation.3 | async-start | bytes 8388608
  268.0 24.6 %slice-start = ((s8[12582912]{0:T(1024)(128)(4,1)}), s8[4194304]{0:T(1024)(128)(4,1)S(1)}, s32[]{:S(2)}) async-start(s8[12582912]{0:T(1024)(128)(4,1)} %bitcast.349), calls=%async_computation | async-start | bytes 8388608
  287.3 26.2 %collective-permute-start.24 = (bf16[768,384]{1,0:T(8,128)(2,1)S(1)}, bf16[768,384]{1,0:T(8,128)(2,1)S(1)}, u32[]{:S(2)}, u32[]{:S(2)}) collective-permute-start(bf16[768,384]{1,0:T(8,128)(2,1)S(1)} %copy-done.67), channel_id=1, source_target_pairs={{0,1},{1,0},{2,3},{3,2},{4,5},{5,4},{6,7},{7,6},{8,9},{9,8},{10,11... | collective-permute-start | bytes 1769480 | tf_op jit(solution)/shard_map/ppermute | solution.py:14
  290.8 135.8 %collective-permute-start.34 = (bf16[3072,384]{1,0:T(8,128)(2,1)}, bf16[3072,384]{1,0:T(8,128)(2,1)}, u32[]{:S(2)}, u32[]{:S(2)}) collective-permute-start(bf16[3072,384]{1,0:T(8,128)(2,1)} %convolution_convert_fusion.1), channel_id=1, source_target_pairs={{0,1},{1,0},{2,3},{3,2},{4,5},{5,4},{6,7},{7,6},{8,9},{9,8},{10,11... | collective-permute-start | bytes 7077896 | tf_op jit(solution)/shard_map/ppermute | solution.py:14
  290.9 156.4 %collective-permute-start.29 = (bf16[768,1536]{1,0:T(8,128)(2,1)}, bf16[768,1536]{1,0:T(8,128)(2,1)}, u32[]{:S(2)}, u32[]{:S(2)}) collective-permute-start(bf16[768,1536]{1,0:T(8,128)(2,1)} %convolution_convert_fusion.2), channel_id=1, source_target_pairs={{0,1},{1,0},{2,3},{3,2},{4,5},{5,4},{6,7},{7,6},{8,9},{9,8},{10,11... | collective-permute-start | bytes 7077896 | tf_op jit(solution)/shard_map/ppermute | solution.py:14
  292.4 23.7 %collective-permute-start.14 = (bf16[768,384]{1,0:T(8,128)(2,1)S(1)}, bf16[768,384]{1,0:T(8,128)(2,1)S(1)}, u32[]{:S(2)}, u32[]{:S(2)}) collective-permute-start(bf16[768,384]{1,0:T(8,128)(2,1)S(1)} %copy-done.68), channel_id=1, source_target_pairs={{0,1},{1,0},{2,3},{3,2},{4,5},{5,4},{6,7},{7,6},{8,9},{9,8},{10,11... | collective-permute-start | bytes 1769480 | tf_op jit(solution)/shard_map/ppermute | solution.py:14
  309.8 110.5 %collective-permute-start.19 = (bf16[768,1152]{1,0:T(8,128)(2,1)}, bf16[768,1152]{1,0:T(8,128)(2,1)}, u32[]{:S(2)}, u32[]{:S(2)}) collective-permute-start(bf16[768,1152]{1,0:T(8,128)(2,1)} %convolution_convert_fusion.3), channel_id=1, source_target_pairs={{0,1},{1,0},{2,3},{3,2},{4,5},{5,4},{6,7},{7,6},{8,9},{9,8},{10,11... | collective-permute-start | bytes 5308424 | tf_op jit(solution)/shard_map/ppermute | solution.py:14
  313.4 5.1 collective-permute-start.4
  316.1 9.5 %collective-permute-start.25 = (bf16[2,2,96,384]{3,2,1,0:T(8,128)(2,1)}, bf16[2,2,96,384]{3,2,1,0:T(8,128)(2,1)}, u32[]{:S(2)}, u32[]{:S(2)}) collective-permute-start(bf16[2,2,96,384]{3,2,1,0:T(8,128)(2,1)} %fusion.131), channel_id=1, source_target_pairs={{0,4},{1,5},{2,6},{3,7},{4,0},{5,1},{6,2},{7,3},{8,12},{9,13},{10,... | collective-permute-start | bytes 884744 | tf_op jit(solution)/shard_map/ppermute | solution.py:14
  318.5 9.5 %collective-permute-start.15 = (bf16[2,2,96,384]{3,2,1,0:T(8,128)(2,1)}, bf16[2,2,96,384]{3,2,1,0:T(8,128)(2,1)}, u32[]{:S(2)}, u32[]{:S(2)}) collective-permute-start(bf16[2,2,96,384]{3,2,1,0:T(8,128)(2,1)} %fusion.130), channel_id=1, source_target_pairs={{0,2},{1,3},{2,0},{3,1},{4,6},{5,7},{6,4},{7,5},{8,10},{9,11},{10,... | collective-permute-start | bytes 884744 | tf_op jit(solution)/shard_map/ppermute | solution.py:14
  322.7 24.2 %copy-start.40 = (f32[768,384]{1,0:T(8,128)S(1)}, f32[768,384]{1,0:T(8,128)}, u32[]{:S(2)}) copy-start(f32[768,384]{1,0:T(8,128)} %copy.106) | copy-start | bytes 3538948
  323.9 24.8 %copy-start.60 = (f32[1536,384]{1,0:T(8,128)S(1)}, f32[1536,384]{1,0:T(8,128)}, u32[]{:S(2)}) copy-start(f32[1536,384]{1,0:T(8,128)} %copy-done.59) | copy-start | bytes 7077892
  325.6 21.4 %collective-permute-start.40 = (bf16[2,2,192,384]{3,2,1,0:T(8,128)(2,1)}, bf16[2,2,192,384]{3,2,1,0:T(8,128)(2,1)S(1)}, u32[]{:S(2)}, u32[]{:S(2)}) collective-permute-start(bf16[2,2,192,384]{3,2,1,0:T(8,128)(2,1)} %fusion.107), channel_id=1, source_target_pairs={{0,2},{1,3},{2,0},{3,1},{4,6},{5,7},{6,4},{7,5},{8,10},{9,11},{10,... | collective-permute-start | bytes 1769480 | tf_op jit(solution)/shard_map/ppermute | solution.py:14
  328.1 18.8 %collective-permute-start.5 = (bf16[2,2,96,384]{3,2,1,0:T(8,128)(2,1)S(1)}, bf16[2,2,96,384]{3,2,1,0:T(8,128)(2,1)S(1)}, u32[]{:S(2)}, u32[]{:S(2)}) collective-permute-start(bf16[2,2,96,384]{3,2,1,0:T(8,128)(2,1)S(1)} %fusion.128), channel_id=1, source_target_pairs={{0,2},{1,3},{2,0},{3,1},{4,6},{5,7},{6,4},{7,5},{8,10},{9,11},{10,... | collective-permute-start | bytes 884744 | tf_op jit(solution)/shard_map/ppermute | solution.py:14
  346.9 8.6 %collective-permute-start.26 = (bf16[2,96,384]{2,1,0:T(8,128)(2,1)S(1)}, bf16[2,96,384]{2,1,0:T(8,128)(2,1)S(1)}, u32[]{:S(2)}, u32[]{:S(2)}) collective-permute-start(bf16[2,96,384]{2,1,0:T(8,128)(2,1)S(1)} %fusion.139), channel_id=1, source_target_pairs={{0,8},{1,9},{2,10},{3,11},{4,12},{5,13},{6,14},{7,15},{8,0},{9,1},... | collective-permute-start | bytes 442376 | tf_op jit(solution)/shard_map/ppermute | solution.py:14
  347.0 8.1 %collective-permute-start.16 = (bf16[2,96,384]{2,1,0:T(8,128)(2,1)S(1)}, bf16[2,96,384]{2,1,0:T(8,128)(2,1)S(1)}, u32[]{:S(2)}, u32[]{:S(2)}) collective-permute-start(bf16[2,96,384]{2,1,0:T(8,128)(2,1)S(1)} %fusion.138), channel_id=1, source_target_pairs={{0,4},{1,5},{2,6},{3,7},{4,0},{5,1},{6,2},{7,3},{8,12},{9,13},{10,... | collective-permute-start | bytes 442376 | tf_op jit(solution)/shard_map/ppermute | solution.py:14
  348.9 33.9 %copy-start.58 = (bf16[512,1536]{0,1:T(8,128)(2,1)S(1)}, bf16[512,1536]{0,1:T(8,128)(2,1)}, u32[]{:S(2)}) copy-start(bf16[512,1536]{0,1:T(8,128)(2,1)} %pad_maximum_fusion.2) | copy-start | bytes 4718596
  355.1 6.7 %collective-permute-start.6 = (bf16[2,96,384]{2,1,0:T(8,128)(2,1)S(1)}, bf16[2,96,384]{2,1,0:T(8,128)(2,1)S(1)}, u32[]{:S(2)}, u32[]{:S(2)}) collective-permute-start(bf16[2,96,384]{2,1,0:T(8,128)(2,1)S(1)} %fusion.136), channel_id=1, source_target_pairs={{0,4},{1,5},{2,6},{3,7},{4,0},{5,1},{6,2},{7,3},{8,12},{9,13},{10,... | collective-permute-start | bytes 442376 | tf_op jit(solution)/shard_map/ppermute | solution.py:14
  355.5 29.0 %collective-permute-start.41 = (bf16[2,192,384]{2,1,0:T(8,128)(2,1)S(1)}, bf16[2,192,384]{2,1,0:T(8,128)(2,1)S(1)}, u32[]{:S(2)}, u32[]{:S(2)}) collective-permute-start(bf16[2,192,384]{2,1,0:T(8,128)(2,1)S(1)} %fusion.134), channel_id=1, source_target_pairs={{0,4},{1,5},{2,6},{3,7},{4,0},{5,1},{6,2},{7,3},{8,12},{9,13},{10,... | collective-permute-start | bytes 884744 | tf_op jit(solution)/shard_map/ppermute | solution.py:14
  361.8 4.4 collective-permute-start.27
  366.2 7.0 %collective-permute-start.17 = (bf16[96,384]{1,0:T(8,128)(2,1)S(1)}, bf16[96,384]{1,0:T(8,128)(2,1)S(1)}, u32[]{:S(2)}, u32[]{:S(2)}) collective-permute-start(bf16[96,384]{1,0:T(8,128)(2,1)S(1)} %fusion.146), channel_id=1, source_target_pairs={{0,8},{1,9},{2,10},{3,11},{4,12},{5,13},{6,14},{7,15},{8,0},{9,1},... | collective-permute-start | bytes 221192 | tf_op jit(solution)/shard_map/ppermute | solution.py:14
  373.2 6.0 %collective-permute-start.7 = (bf16[96,384]{1,0:T(8,128)(2,1)S(1)}, bf16[96,384]{1,0:T(8,128)(2,1)S(1)}, u32[]{:S(2)}, u32[]{:S(2)}) collective-permute-start(bf16[96,384]{1,0:T(8,128)(2,1)S(1)} %fusion.144), channel_id=1, source_target_pairs={{0,8},{1,9},{2,10},{3,11},{4,12},{5,13},{6,14},{7,15},{8,0},{9,1},... | collective-permute-start | bytes 221192 | tf_op jit(solution)/shard_map/ppermute | solution.py:14
  379.2 1.2 collective-permute-start.28
  380.4 1.2 collective-permute-start.18
  381.6 1.2 collective-permute-start.8
  382.8 36.5 %collective-permute-start.3 = (bf16[512,1536]{0,1:T(8,128)(2,1)S(1)}, bf16[512,1536]{0,1:T(8,128)(2,1)S(1)}, u32[]{:S(2)}, u32[]{:S(2)}) collective-permute-start(bf16[512,1536]{0,1:T(8,128)(2,1)S(1)} %copy-done.58), channel_id=1, source_target_pairs={{0,16},{16,0},{1,17},{17,1},{2,18},{18,2},{3,19},{19,3},{4,20},{20... | collective-permute-start | bytes 4718600 | tf_op jit(solution)/shard_map/ppermute | solution.py:14
  384.4 34.9 %copy-start.18 = (bf16[1,512,768]{2,1,0:T(8,128)(2,1)S(1)}, bf16[1,512,768]{2,1,0:T(8,128)(2,1)}, u32[]{:S(2)}) copy-start(bf16[1,512,768]{2,1,0:T(8,128)(2,1)} %param.15) | copy-start | bytes 2359300
  384.5 9.6 %collective-permute-start.42 = (bf16[192,384]{1,0:T(8,128)(2,1)S(1)}, bf16[192,384]{1,0:T(8,128)(2,1)S(1)}, u32[]{:S(2)}, u32[]{:S(2)}) collective-permute-start(bf16[192,384]{1,0:T(8,128)(2,1)S(1)} %fusion.142), channel_id=1, source_target_pairs={{0,8},{1,9},{2,10},{3,11},{4,12},{5,13},{6,14},{7,15},{8,0},{9,1},... | collective-permute-start | bytes 442376 | tf_op jit(solution)/shard_map/ppermute | solution.py:14
  394.2 1.3 collective-permute-start.43
  394.3 26.0 %copy-start.30 = (bf16[512,2304]{0,1:T(8,128)(2,1)S(1)}, bf16[512,2304]{0,1:T(8,128)(2,1)}, u32[]{:S(2)}) copy-start(bf16[512,2304]{0,1:T(8,128)(2,1)} %pad_maximum_fusion) | copy-start | bytes 7077892
  394.3 26.0 %copy-start.36 = (bf16[512,768]{1,0:T(8,128)(2,1)S(1)}, bf16[512,768]{1,0:T(8,128)(2,1)}, u32[]{:S(2)}) copy-start(bf16[512,768]{1,0:T(8,128)(2,1)} %copy-done.34) | copy-start | bytes 2359300
  420.2 48.2 %collective-permute-start.9 = (bf16[768,768]{1,0:T(8,128)(2,1)S(1)}, bf16[768,768]{1,0:T(8,128)(2,1)S(1)}, u32[]{:S(2)}, u32[]{:S(2)}) collective-permute-start(bf16[768,768]{1,0:T(8,128)(2,1)S(1)} %fusion.67), channel_id=1, source_target_pairs={{0,1},{1,0},{2,3},{3,2},{4,5},{5,4},{6,7},{7,6},{8,9},{9,8},{10,11... | collective-permute-start | bytes 3538952 | tf_op jit(solution)/shard_map/ppermute | solution.py:14
  423.5 22.3 %collective-permute-start.20 = (bf16[2,2,96,1152]{3,2,1,0:T(8,128)(2,1)S(1)}, bf16[2,2,96,1152]{3,2,1,0:T(8,128)(2,1)S(1)}, u32[]{:S(2)}, u32[]{:S(2)}) collective-permute-start(bf16[2,2,96,1152]{3,2,1,0:T(8,128)(2,1)S(1)} %fusion.93), channel_id=1, source_target_pairs={{0,4},{1,5},{2,6},{3,7},{4,0},{5,1},{6,2},{7,3},{8,12},{9,13},{10,... | collective-permute-start | bytes 2654216 | tf_op jit(solution)/shard_map/ppermute | solution.py:14
  430.3 73.9 %collective-permute-start.35 = (bf16[2,2,384,384]{3,2,1,0:T(8,128)(2,1)S(1)}, bf16[2,2,384,384]{3,2,1,0:T(8,128)(2,1)S(1)}, u32[]{:S(2)}, u32[]{:S(2)}) collective-permute-start(bf16[2,2,384,384]{3,2,1,0:T(8,128)(2,1)S(1)} %fusion.80), channel_id=1, source_target_pairs={{0,2},{1,3},{2,0},{3,1},{4,6},{5,7},{6,4},{7,5},{8,10},{9,11},{10,... | collective-permute-start | bytes 3538952 | tf_op jit(solution)/shard_map/ppermute | solution.py:14
  446.0 22.2 %collective-permute-start.21 = (bf16[2,96,1152]{2,1,0:T(8,128)(2,1)S(1)}, bf16[2,96,1152]{2,1,0:T(8,128)(2,1)S(1)}, u32[]{:S(2)}, u32[]{:S(2)}) collective-permute-start(bf16[2,96,1152]{2,1,0:T(8,128)(2,1)S(1)} %fusion.108), channel_id=1, source_target_pairs={{0,8},{1,9},{2,10},{3,11},{4,12},{5,13},{6,14},{7,15},{8,0},{9,1},... | collective-permute-start | bytes 1327112 | tf_op jit(solution)/shard_map/ppermute | solution.py:14
  450.9 63.5 %collective-permute-start.30 = (bf16[2,2,96,1536]{3,2,1,0:T(8,128)(2,1)S(1)}, bf16[2,2,96,1536]{3,2,1,0:T(8,128)(2,1)S(1)}, u32[]{:S(2)}, u32[]{:S(2)}) collective-permute-start(bf16[2,2,96,1536]{3,2,1,0:T(8,128)(2,1)S(1)} %fusion.79), channel_id=1, source_target_pairs={{0,2},{1,3},{2,0},{3,1},{4,6},{5,7},{6,4},{7,5},{8,10},{9,11},{10,... | collective-permute-start | bytes 3538952 | tf_op jit(solution)/shard_map/ppermute | solution.py:14
  468.3 20.8 %collective-permute-start.22 = (bf16[96,1152]{1,0:T(8,128)(2,1)S(1)}, bf16[96,1152]{1,0:T(8,128)(2,1)S(1)}, u32[]{:S(2)}, u32[]{:S(2)}) collective-permute-start(bf16[96,1152]{1,0:T(8,128)(2,1)S(1)} %fusion.135), channel_id=1, source_target_pairs={{0,2},{1,3},{2,0},{3,1},{4,6},{5,7},{6,4},{7,5},{8,10},{9,11},{10,... | collective-permute-start | bytes 663560 | tf_op jit(solution)/shard_map/ppermute | solution.py:14
  469.4 32.0 %collective-permute-start.10 = (bf16[2,2,96,768]{3,2,1,0:T(8,128)(2,1)S(1)}, bf16[2,2,96,768]{3,2,1,0:T(8,128)(2,1)S(1)}, u32[]{:S(2)}, u32[]{:S(2)}) collective-permute-start(bf16[2,2,96,768]{3,2,1,0:T(8,128)(2,1)S(1)} %fusion.104), channel_id=1, source_target_pairs={{0,2},{1,3},{2,0},{3,1},{4,6},{5,7},{6,4},{7,5},{8,10},{9,11},{10,... | collective-permute-start | bytes 1769480 | tf_op jit(solution)/shard_map/ppermute | solution.py:14
  489.2 14.1 %collective-permute-start.23 = (bf16[48,1152]{1,0:T(8,128)(2,1)S(1)}, bf16[48,1152]{1,0:T(8,128)(2,1)S(1)}, u32[]{:S(2)}, u32[]{:S(2)}) collective-permute-start(bf16[48,1152]{1,0:T(8,128)(2,1)S(1)} %fusion.143), channel_id=1, source_target_pairs={{0,1},{1,0},{2,3},{3,2},{4,5},{5,4},{6,7},{7,6},{8,9},{9,8},{10,11... | collective-permute-start | bytes 331784 | tf_op jit(solution)/shard_map/ppermute | solution.py:14
  501.5 10.0 %collective-permute-start.11 = (bf16[2,96,768]{2,1,0:T(8,128)(2,1)S(1)}, bf16[2,96,768]{2,1,0:T(8,128)(2,1)S(1)}, u32[]{:S(2)}, u32[]{:S(2)}) collective-permute-start(bf16[2,96,768]{2,1,0:T(8,128)(2,1)S(1)} %fusion.129), channel_id=1, source_target_pairs={{0,4},{1,5},{2,6},{3,7},{4,0},{5,1},{6,2},{7,3},{8,12},{9,13},{10,... | collective-permute-start | bytes 884744 | tf_op jit(solution)/shard_map/ppermute | solution.py:14
  504.4 25.2 %collective-permute-start.36 = (bf16[2,384,384]{2,1,0:T(8,128)(2,1)S(1)}, bf16[2,384,384]{2,1,0:T(8,128)(2,1)S(1)}, u32[]{:S(2)}, u32[]{:S(2)}) collective-permute-start(bf16[2,384,384]{2,1,0:T(8,128)(2,1)S(1)} %fusion.106), channel_id=1, source_target_pairs={{0,4},{1,5},{2,6},{3,7},{4,0},{5,1},{6,2},{7,3},{8,12},{9,13},{10,... | collective-permute-start | bytes 1769480 | tf_op jit(solution)/shard_map/ppermute | solution.py:14
  511.6 13.5 %collective-permute-start.12 = (bf16[96,768]{1,0:T(8,128)(2,1)S(1)}, bf16[96,768]{1,0:T(8,128)(2,1)S(1)}, u32[]{:S(2)}, u32[]{:S(2)}) collective-permute-start(bf16[96,768]{1,0:T(8,128)(2,1)S(1)} %fusion.137), channel_id=1, source_target_pairs={{0,8},{1,9},{2,10},{3,11},{4,12},{5,13},{6,14},{7,15},{8,0},{9,1},... | collective-permute-start | bytes 442376 | tf_op jit(solution)/shard_map/ppermute | solution.py:14
  525.2 3.7 collective-permute-start.13
  525.3 23.9 %collective-permute-start.31 = (bf16[2,96,1536]{2,1,0:T(8,128)(2,1)S(1)}, bf16[2,96,1536]{2,1,0:T(8,128)(2,1)S(1)}, u32[]{:S(2)}, u32[]{:S(2)}) collective-permute-start(bf16[2,96,1536]{2,1,0:T(8,128)(2,1)S(1)} %fusion.105), channel_id=1, source_target_pairs={{0,4},{1,5},{2,6},{3,7},{4,0},{5,1},{6,2},{7,3},{8,12},{9,13},{10,... | collective-permute-start | bytes 1769480 | tf_op jit(solution)/shard_map/ppermute | solution.py:14
  529.8 19.6 %collective-permute-start.37 = (bf16[384,384]{1,0:T(8,128)(2,1)S(1)}, bf16[384,384]{1,0:T(8,128)(2,1)S(1)}, u32[]{:S(2)}, u32[]{:S(2)}) collective-permute-start(bf16[384,384]{1,0:T(8,128)(2,1)S(1)} %fusion.133), channel_id=1, source_target_pairs={{0,8},{1,9},{2,10},{3,11},{4,12},{5,13},{6,14},{7,15},{8,0},{9,1},... | collective-permute-start | bytes 884744 | tf_op jit(solution)/shard_map/ppermute | solution.py:14
  549.4 15.1 %collective-permute-start.32 = (bf16[96,1536]{1,0:T(8,128)(2,1)S(1)}, bf16[96,1536]{1,0:T(8,128)(2,1)S(1)}, u32[]{:S(2)}, u32[]{:S(2)}) collective-permute-start(bf16[96,1536]{1,0:T(8,128)(2,1)S(1)} %fusion.132), channel_id=1, source_target_pairs={{0,8},{1,9},{2,10},{3,11},{4,12},{5,13},{6,14},{7,15},{8,0},{9,1},... | collective-permute-start | bytes 884744 | tf_op jit(solution)/shard_map/ppermute | solution.py:14
  549.6 15.1 %collective-permute-start.38 = (bf16[192,384]{1,0:T(8,128)(2,1)S(1)}, bf16[192,384]{1,0:T(8,128)(2,1)S(1)}, u32[]{:S(2)}, u32[]{:S(2)}) collective-permute-start(bf16[192,384]{1,0:T(8,128)(2,1)S(1)} %fusion.141), channel_id=1, source_target_pairs={{0,1},{1,0},{2,3},{3,2},{4,5},{5,4},{6,7},{7,6},{8,9},{9,8},{10,11... | collective-permute-start | bytes 442376 | tf_op jit(solution)/shard_map/ppermute | solution.py:14
  564.6 1.4 collective-permute-start.33
  (113 other events, 630.5 us)
